TPU v7x, 32 devices: a whole 2x2x4 slice. The times are simulated.
32 devices in a mesh: dp: 16 (over z, y, core), tensor: 2 (over x).
Axes of the slice: x: 2, y: 2, z: 4, core: 2. Of those that a mesh axis runs over, the one named last changes fastest.
Arguments:
- tokens: bfloat16 [32768, 1024], P(('dp', 'tensor')), may hold values from -6 to 6
- scene_ids: int32 [16, 2048], P('dp'), may hold values from 0 to 3, never falling along the last dimension, each value on 1 to 1024 neighbouring positions
- valid: int32 [16, 2048], P('dp'), may hold values 0 or 1
- norm_gain: bfloat16 [1024], replicated, may hold values from 0.5 to 1.5
- w_z: bfloat16 [1024, 2048], P(None, 'tensor'), may hold values from -0.1875 to 0.1875
- w_x: bfloat16 [1024, 2048], P(None, 'tensor'), may hold values from -0.1875 to 0.1875
- w_b: bfloat16 [1024, 128], replicated, may hold values from -0.1875 to 0.1875
- w_c: bfloat16 [1024, 128], replicated, may hold values from -0.1875 to 0.1875
- w_dt: bfloat16 [1024, 32], P(None, 'tensor'), may hold values from -0.1875 to 0.1875
- conv_x: bfloat16 [4, 2048], P(None, 'tensor'), may hold values from -3 to 3
- conv_x_bias: bfloat16 [2048], P('tensor'), may hold values from -3 to 3
- conv_bc: bfloat16 [4, 256], replicated, may hold values from -3 to 3
- conv_bc_bias: bfloat16 [256], replicated, may hold values from -3 to 3
- dt_bias: bfloat16 [32], P('tensor'), may hold values from -9 to -3.5
- a_log: bfloat16 [32], P('tensor'), may hold values from 0 to 2.765625
- d_skip: bfloat16 [32], P('tensor'), may hold values from 0.5 to 1.5
- gate_gain: bfloat16 [2048], P('tensor'), may hold values from 0.5 to 1.5
- w_out: bfloat16 [2048, 1024], P('tensor'), may hold values from -0.125 to 0.125
- cotangent: bfloat16 [32768, 1024], P(('dp', 'tensor')), may hold values from -6 to 6
Outputs:
- block_out: bfloat16 [32768, 1024], P(('dp', 'tensor'))
- grad_tokens: bfloat16 [32768, 1024], P(('dp', 'tensor'))
- grad_norm_gain: float32 [1024], replicated
- grad_w_z: float32 [1024, 2048], P(None, 'tensor')
- grad_w_x: float32 [1024, 2048], P(None, 'tensor')
- grad_w_b: float32 [1024, 128], replicated
- grad_w_c: float32 [1024, 128], replicated
- grad_w_dt: float32 [1024, 32], P(None, 'tensor')
- grad_conv_x: float32 [4, 2048], P(None, 'tensor')
- grad_conv_x_bias: float32 [2048], P('tensor')
- grad_conv_bc: float32 [4, 256], replicated
- grad_conv_bc_bias: float32 [256], replicated
- grad_dt_bias: float32 [32], P('tensor')
- grad_a_log: float32 [32], P('tensor')
- grad_d_skip: float32 [32], P('tensor')
- grad_gate_gain: float32 [2048], P('tensor')
- grad_w_out: float32 [2048, 1024], P('tensor')
Inputs may be any that keep to these rules, and one draw needn't show every extreme that they name: `scene_ids`: each packed row of 2048 holds 4 scenes one after another, numbered from 0 up, each of 1 to 1024 rows, one of exactly 1024.
All inputs are finite; a program needn't handle non-finite values. No bound on the sum of `valid` on one device may be relied on, other than what follows from the above.
Results may differ from a plain program's by a relative error of at most 0.0081.
Values may be sent and summed in bfloat16 or wider, within the bound.
No kernel may reach another device: no remote copies, remote signals or barrier semaphores. Data moves between devices by JAX's collectives and lax.ppermute only.
A program may use at most 256 MiB of HBM per device.

v0:
```python
import jax
import jax.numpy as jnp
from jax import lax
from jax.sharding import PartitionSpec as P

SPAN = 512


EPSILON = 1e-05


def causal_conv(values, kernel, bias_row, scene_row):
    tap_count = kernel.shape[0]
    result = bias_row[None, :] + kernel[tap_count - 1][None, :] * values
    for lag_rows in range(1, tap_count):
        shifted = jnp.pad(values[:-lag_rows], ((lag_rows, 0), (0, 0)))
        earlier = jnp.pad(scene_row[:-lag_rows], (lag_rows, 0), constant_values=-1)
        same_scene = (earlier == scene_row).astype(jnp.float32)[:, None]
        result = result + kernel[tap_count - 1 - lag_rows][None, :] * shifted * same_scene
    return result


def ssd_scan(x_heads, dt_step, log_decay, b_matrix, c_matrix, scene_row, d_skip):
    row_total, head_count, head_width = x_heads.shape
    block_count = row_total // SPAN
    highest = lax.Precision.HIGHEST

    def block_step(carry_pair, block_items):
        carried_state, prev_seg = carry_pair
        x_block, step_block, decay_block, b_block, c_block, seg_block = block_items
        cumulative = jnp.cumsum(decay_block, axis=0)
        positions = jnp.arange(SPAN)
        causal_mask = (positions[:, None] >= positions[None, :]) & (
            seg_block[:, None] == seg_block[None, :]
        )
        log_gap = cumulative[:, None, :] - cumulative[None, :, :]
        weight = jnp.where(
            causal_mask[:, :, None], jnp.exp(jnp.where(causal_mask[:, :, None], log_gap, 0.0)), 0.0
        )
        scores = jnp.dot(c_block, b_block.T, precision=highest)
        mixing = weight * scores[:, :, None] * step_block[None, :, :]
        inner_part = jnp.einsum("ijh,jhp->ihp", mixing, x_block, precision=highest)
        carried = (seg_block == prev_seg).astype(jnp.float32)
        from_state = jnp.einsum("in,hnp->ihp", c_block, carried_state, precision=highest)
        from_state = from_state * (jnp.exp(cumulative) * carried[:, None])[:, :, None]
        block_out = inner_part + from_state + d_skip[None, :, None] * x_block
        last_seg = seg_block[-1]
        tail_weight = (
            jnp.exp(cumulative[-1][None, :] - cumulative)
            * step_block
            * (seg_block == last_seg).astype(jnp.float32)[:, None]
        )
        keep_factor = jnp.exp(cumulative[-1]) * (last_seg == prev_seg).astype(jnp.float32)
        new_state = keep_factor[:, None, None] * carried_state + jnp.einsum(
            "jh,jn,jhp->hnp", tail_weight, b_block, x_block, precision=highest
        )
        return ((new_state, last_seg), block_out)

    state_init = jnp.zeros((head_count, b_matrix.shape[1], head_width), jnp.float32)
    block_items = (
        x_heads.reshape(block_count, SPAN, head_count, head_width),
        dt_step.reshape(block_count, SPAN, head_count),
        log_decay.reshape(block_count, SPAN, head_count),
        b_matrix.reshape(block_count, SPAN, -1),
        c_matrix.reshape(block_count, SPAN, -1),
        scene_row.reshape(block_count, SPAN),
    )
    final_pair, outputs = lax.scan(
        jax.checkpoint(block_step), (state_init, jnp.array(-1, jnp.int32)), block_items
    )
    return outputs.reshape(row_total, head_count, head_width)


def mixer(
    x_raw,
    bc_raw,
    dt_raw,
    conv_x,
    conv_x_bias,
    conv_bc,
    conv_bc_bias,
    dt_bias,
    a_log,
    d_skip,
    scene_row,
    live_row,
):
    x_conv = jax.nn.silu(causal_conv(x_raw, conv_x, conv_x_bias, scene_row)) * live_row[:, None]
    bc_conv = jax.nn.silu(causal_conv(bc_raw, conv_bc, conv_bc_bias, scene_row))
    half_state = bc_conv.shape[1] // 2
    dt_step = jax.nn.softplus(dt_raw + dt_bias[None, :]) * live_row[:, None]
    log_decay = -jnp.exp(a_log)[None, :] * dt_step
    head_count = dt_raw.shape[1]
    x_heads = x_conv.reshape(x_conv.shape[0], head_count, -1)
    mixed = ssd_scan(
        x_heads,
        dt_step,
        log_decay,
        bc_conv[:, :half_state],
        bc_conv[:, half_state:],
        scene_row,
        d_skip,
    )
    return mixed.reshape(x_conv.shape[0], -1)


def contract_rows(left_side, right_side):
    return lax.dot_general(
        left_side, right_side, (((0,), (0,)), ((), ())), preferred_element_type=jnp.float32
    )


def contract_cols(left_side, right_side):
    return lax.dot_general(
        left_side, right_side, (((1,), (1,)), ((), ())), preferred_element_type=jnp.float32
    )


def shards(
    tokens,
    scene_ids,
    valid,
    norm_gain,
    w_z,
    w_x,
    w_b,
    w_c,
    w_dt,
    conv_x,
    conv_x_bias,
    conv_bc,
    conv_bc_bias,
    dt_bias,
    a_log,
    d_skip,
    gate_gain,
    w_out,
    cotangent,
):
    rows_own = tokens.shape[0]
    model_width = tokens.shape[1]
    head_cols = w_z.shape[1]
    state_cols = w_b.shape[1]
    inner_width = head_cols * lax.axis_size("tensor")
    scene_row = scene_ids[0]
    live_row = valid[0].astype(jnp.float32)
    row_start = lax.axis_index("tensor") * rows_own
    live_own = lax.dynamic_slice_in_dim(live_row, row_start, rows_own)
    resid = tokens.astype(jnp.float32)
    gain_in = norm_gain.astype(jnp.float32)[None, :]
    inverse_in = lax.rsqrt(jnp.mean(resid * resid, axis=1, keepdims=True) + EPSILON)
    normed_own = (resid * inverse_in * gain_in).astype(jnp.bfloat16)
    normed_all = lax.all_gather(normed_own, "tensor", axis=0, tiled=True)
    head_weight = jnp.concatenate([w_z, w_x, w_dt], axis=1)
    shared_weight = jnp.concatenate([w_b, w_c], axis=1)
    projected = jnp.dot(normed_all, head_weight, preferred_element_type=jnp.float32)
    gate_raw = projected[:, :head_cols]
    x_raw = projected[:, head_cols : 2 * head_cols]
    dt_raw = projected[:, 2 * head_cols :]
    bc_raw = jnp.dot(normed_all, shared_weight, preferred_element_type=jnp.float32)
    small_params = tuple(
        (
            member.astype(jnp.float32)
            for member in (conv_x, conv_x_bias, conv_bc, conv_bc_bias, dt_bias, a_log, d_skip)
        )
    )

    def local_mixer(x_input, bc_input, dt_input, *params):
        return mixer(x_input, bc_input, dt_input, *params, scene_row, live_row)

    mixed, mixer_pullback = jax.vjp(local_mixer, x_raw, bc_raw, dt_raw, *small_params)
    gate_sig = jax.nn.sigmoid(gate_raw)
    gate_silu = gate_raw * gate_sig
    gated = mixed * gate_silu
    row_squares = lax.psum(jnp.sum(gated * gated, axis=1), "tensor")
    inverse_gate = lax.rsqrt(row_squares / inner_width + EPSILON)[:, None]
    gain_gate = gate_gain.astype(jnp.float32)[None, :]
    normed_gate = (gated * inverse_gate * gain_gate).astype(jnp.bfloat16)
    branch = lax.psum_scatter(
        jnp.dot(normed_gate, w_out, preferred_element_type=jnp.float32),
        "tensor",
        scatter_dimension=0,
        tiled=True,
    )
    block_out = (resid + live_own[:, None] * branch).astype(jnp.bfloat16)
    cot_float = cotangent.astype(jnp.float32)
    branch_grad = (cot_float * live_own[:, None]).astype(jnp.bfloat16)
    branch_all = lax.all_gather(branch_grad, "tensor", axis=0, tiled=True)
    grad_w_out = contract_rows(normed_gate, branch_all)
    normed_grad = contract_cols(branch_all, w_out)
    grad_gate_gain = jnp.sum(normed_grad * gated * inverse_gate, axis=0)
    row_dots = lax.psum(jnp.sum(normed_grad * gain_gate * gated, axis=1), "tensor")
    gated_grad = (
        normed_grad * gain_gate * inverse_gate
        - gated * inverse_gate**3 * (row_dots / inner_width)[:, None]
    )
    mixed_grad = gated_grad * gate_silu
    gate_grad = gated_grad * mixed * gate_sig * (1.0 + gate_raw * (1.0 - gate_sig))
    mixer_grads = mixer_pullback(mixed_grad)
    head_grad = jnp.concatenate([gate_grad, mixer_grads[0], mixer_grads[2]], axis=1).astype(
        jnp.bfloat16
    )
    shared_grad = lax.psum_scatter(
        mixer_grads[1], "tensor", scatter_dimension=0, tiled=True
    ).astype(jnp.bfloat16)
    grad_head_weight = contract_rows(normed_all, head_grad)
    normed_in_grad = lax.psum_scatter(
        contract_cols(head_grad, head_weight), "tensor", scatter_dimension=0, tiled=True
    )
    normed_in_grad = normed_in_grad + contract_cols(shared_grad, shared_weight)
    grad_norm_part = jnp.sum(normed_in_grad * resid * inverse_in, axis=0)
    row_inner = jnp.sum(gain_in * normed_in_grad * resid, axis=1, keepdims=True)
    input_grad = (
        cot_float
        + inverse_in * gain_in * normed_in_grad
        - resid * inverse_in**3 * (row_inner / model_width)
    )
    grad_shared_weight = contract_rows(normed_own, shared_grad)
    head_sums = lax.psum(
        (
            grad_head_weight,
            grad_w_out,
            mixer_grads[3],
            mixer_grads[4],
            mixer_grads[7],
            mixer_grads[8],
            mixer_grads[9],
            grad_gate_gain,
        ),
        "dp",
    )
    shared_sums = lax.psum(
        (grad_shared_weight, mixer_grads[5], mixer_grads[6], grad_norm_part), ("dp", "tensor")
    )
    summed_head = head_sums[0]
    summed_shared = shared_sums[0]
    return (
        block_out,
        input_grad.astype(jnp.bfloat16),
        shared_sums[3],
        summed_head[:, :head_cols],
        summed_head[:, head_cols : 2 * head_cols],
        summed_shared[:, :state_cols],
        summed_shared[:, state_cols:],
        summed_head[:, 2 * head_cols :],
        head_sums[2],
        head_sums[3],
        shared_sums[1],
        shared_sums[2],
        head_sums[4],
        head_sums[5],
        head_sums[6],
        head_sums[7],
        head_sums[1],
    )


def solution(mesh):
    in_specs = (
        P(("dp", "tensor"), None),
        P("dp", None),
        P("dp", None),
        P(),
        P(None, "tensor"),
        P(None, "tensor"),
        P(),
        P(),
        P(None, "tensor"),
        P(None, "tensor"),
        P("tensor"),
        P(),
        P(),
        P("tensor"),
        P("tensor"),
        P("tensor"),
        P("tensor"),
        P("tensor", None),
        P(("dp", "tensor"), None),
    )
    out_specs = (
        P(("dp", "tensor"), None),
        P(("dp", "tensor"), None),
        P(),
        P(None, "tensor"),
        P(None, "tensor"),
        P(),
        P(),
        P(None, "tensor"),
        P(None, "tensor"),
        P("tensor"),
        P(),
        P(),
        P("tensor"),
        P("tensor"),
        P("tensor"),
        P("tensor"),
        P("tensor", None),
    )
    return jax.shard_map(shards, mesh=mesh, in_specs=in_specs, out_specs=out_specs, check_vma=False)
```

profile of v0, /device:TPU:0, one launch (start us, length us, event | category | flops | bytes accessed | tf_op | source)
XLA Modules:
  0.0 1879.4 jit_solution(6227101494781437763)
XLA Ops:
  24.6 49.9 %all-gather.3.cloned.1.call-done = bf16[2048,1024]{1,0:T(8,128)(2,1)} async-done(((bf16[1024,1024]{1,0:T(8,128)(2,1)}), bf16[2048,1024]{1,0:T(8,128)(2,1)}) %all-gather.3.cloned.1.call-update) | async-done | bytes 4194320 | tf_op jit(solution)/shard_map/all_gather | solution.py:153
  110.7 19.1 %multiply_multiply_fusion.3 = (f32[2048,1024]{0,1:T(8,128)}, f32[2048,1024]{0,1:T(8,128)}) fusion(f32[2048]{0:T(1024)S(1)} %bitcast.473, f32[2048]{0:T(1024)S(1)} %get-tuple-element.962, f32[2045,1024]{0,1:T(8,128)} %slice.234, f32[1024]{0:T(1024)S(1)} %bitcast.486, f32[2048]{0:T(1024)S(1)} %get-tuple-element.963, f32[2046,1024]{0,1:T(8,128)} %slice.232, ...), kind=kLoop, calls=%fused_computation.171 | loop fusion | flops 33554432 | bytes 50360320 | tf_op jit(solution)/shard_map/jvp()/mul | solution.py:88
  164.1 334.4 %while.48 = (s32[]{:T(128)}, f32[16,128,64]{1,2,0:T(8,128)S(1)}, s32[]{:T(128)}, f32[4,512,16,64]{1,0,3,2:T(4,128)}, f32[4,16,128,64]{2,3,1,0:T(8,128)}, /*index...) while((s32[]{:T(128)}, f32[16,128,64]{1,2,0:T(8,128)S(1)}, ...), condition=%wide.region_4.5_spmd.clone, body=%wide.region_1.4_spmd.clone.sunk | while | flops 5260355584 | bytes 28335808 | solution.py:68
  175.9 22.5 %fusion.231 = f32[1,512,16,64]{1,3,2,0:T(8,128)S(1)} fusion(f32[512,16,64]{0,2,1:T(8,128)S(1)} %bitcast.455, f32[4,512,16,64]{1,3,2,0:T(8,128)} %get-tuple-element.1288, s32[]{:T(128)} %get-tuple-element.1262, f32[512,16]{0,1:T(8,128)S(1)} %get-tuple-element.1192, f32[512,512]{1,0:T(8,128)S(1)} %fusion.229, ...), kind=kOutput, calls=%fused_computation.16.clone.1 | convolution fusion | flops 3244294144 | bytes 9831936 | tf_op jit(solution)/shard_map/jvp()/while/body/eval_jaxpr/ijh,jhp->ihp/dot_general | solution.py:42
  201.9 41.0 %dynamic_update_slice.88 = f32[4,512,16,64]{1,0,3,2:T(4,128)} dynamic-update-slice(f32[4,512,16,64]{1,0,3,2:T(4,128)} %get-tuple-element.1265, f32[1,512,16,64]{1,0,3,2:T(1,128)} %copy.214, s32[]{:T(128)} %get-tuple-element.1262, s32[]{:T(128)} %constant.145.clone.1..sunk, s32[]{:T(128)} %constant.145.clone.1..sunk, s32[]{:T(128)} %constant.145.clone.1..sunk) | dynamic-update-slice | bytes 4194308 | tf_op jit(solution)/shard_map/jvp()/while/body/jit(dynamic_update_index_in_dim)/dynamic_update_slice | solution.py:68
  259.5 22.3 %fusion.231 = f32[1,512,16,64]{1,3,2,0:T(8,128)S(1)} fusion(f32[512,16,64]{0,2,1:T(8,128)S(1)} %bitcast.455, f32[4,512,16,64]{1,3,2,0:T(8,128)} %get-tuple-element.1288, s32[]{:T(128)} %get-tuple-element.1262, f32[512,16]{0,1:T(8,128)S(1)} %get-tuple-element.1192, f32[512,512]{1,0:T(8,128)S(1)} %fusion.229, ...), kind=kOutput, calls=%fused_computation.16.clone.1 | convolution fusion | flops 3244294144 | bytes 9831936 | tf_op jit(solution)/shard_map/jvp()/while/body/eval_jaxpr/ijh,jhp->ihp/dot_general | solution.py:42
  285.3 41.0 %dynamic_update_slice.88 = f32[4,512,16,64]{1,0,3,2:T(4,128)} dynamic-update-slice(f32[4,512,16,64]{1,0,3,2:T(4,128)} %get-tuple-element.1265, f32[1,512,16,64]{1,0,3,2:T(1,128)} %copy.214, s32[]{:T(128)} %get-tuple-element.1262, s32[]{:T(128)} %constant.145.clone.1..sunk, s32[]{:T(128)} %constant.145.clone.1..sunk, s32[]{:T(128)} %constant.145.clone.1..sunk) | dynamic-update-slice | bytes 4194308 | tf_op jit(solution)/shard_map/jvp()/while/body/jit(dynamic_update_index_in_dim)/dynamic_update_slice | solution.py:68
  342.9 22.6 %fusion.231 = f32[1,512,16,64]{1,3,2,0:T(8,128)S(1)} fusion(f32[512,16,64]{0,2,1:T(8,128)S(1)} %bitcast.455, f32[4,512,16,64]{1,3,2,0:T(8,128)} %get-tuple-element.1288, s32[]{:T(128)} %get-tuple-element.1262, f32[512,16]{0,1:T(8,128)S(1)} %get-tuple-element.1192, f32[512,512]{1,0:T(8,128)S(1)} %fusion.229, ...), kind=kOutput, calls=%fused_computation.16.clone.1 | convolution fusion | flops 3244294144 | bytes 9831936 | tf_op jit(solution)/shard_map/jvp()/while/body/eval_jaxpr/ijh,jhp->ihp/dot_general | solution.py:42
  369.0 41.0 %dynamic_update_slice.88 = f32[4,512,16,64]{1,0,3,2:T(4,128)} dynamic-update-slice(f32[4,512,16,64]{1,0,3,2:T(4,128)} %get-tuple-element.1265, f32[1,512,16,64]{1,0,3,2:T(1,128)} %copy.214, s32[]{:T(128)} %get-tuple-element.1262, s32[]{:T(128)} %constant.145.clone.1..sunk, s32[]{:T(128)} %constant.145.clone.1..sunk, s32[]{:T(128)} %constant.145.clone.1..sunk) | dynamic-update-slice | bytes 4194308 | tf_op jit(solution)/shard_map/jvp()/while/body/jit(dynamic_update_index_in_dim)/dynamic_update_slice | solution.py:68
  426.5 22.5 %fusion.231 = f32[1,512,16,64]{1,3,2,0:T(8,128)S(1)} fusion(f32[512,16,64]{0,2,1:T(8,128)S(1)} %bitcast.455, f32[4,512,16,64]{1,3,2,0:T(8,128)} %get-tuple-element.1288, s32[]{:T(128)} %get-tuple-element.1262, f32[512,16]{0,1:T(8,128)S(1)} %get-tuple-element.1192, f32[512,512]{1,0:T(8,128)S(1)} %fusion.229, ...), kind=kOutput, calls=%fused_computation.16.clone.1 | convolution fusion | flops 3244294144 | bytes 9831936 | tf_op jit(solution)/shard_map/jvp()/while/body/eval_jaxpr/ijh,jhp->ihp/dot_general | solution.py:42
  452.5 41.0 %dynamic_update_slice.88 = f32[4,512,16,64]{1,0,3,2:T(4,128)} dynamic-update-slice(f32[4,512,16,64]{1,0,3,2:T(4,128)} %get-tuple-element.1265, f32[1,512,16,64]{1,0,3,2:T(1,128)} %copy.214, s32[]{:T(128)} %get-tuple-element.1262, s32[]{:T(128)} %constant.145.clone.1..sunk, s32[]{:T(128)} %constant.145.clone.1..sunk, s32[]{:T(128)} %constant.145.clone.1..sunk) | dynamic-update-slice | bytes 4194308 | tf_op jit(solution)/shard_map/jvp()/while/body/jit(dynamic_update_index_in_dim)/dynamic_update_slice | solution.py:68
  537.4 17.9 multiply_convert_fusion
  574.7 606.5 %while.49 = (s32[]{:T(128)}, f32[16]{0:T(128)}, f32[16,128,64]{1,2,0:T(8,128)}, f32[4,512,16,64]{1,0,3,2:T(4,128)}, f32[4,512,16]{1,0,2:T(4,128)}, /*index=5*/f3...) while((s32[]{:T(128)}, f32[16]{0:T(128)}, ...), condition=%wide.region_23.24_spmd.clone, body=%wide.region_10.23_spmd.clone.sunk | while | flops 11771217920 | bytes 107105008 | solution.py:68
  608.6 27.1 %fusion.256 = (f32[512,16]{0,1:T(8,128)S(1)}, f32[512,16]{0,1:T(8,128)S(1)}, f32[512,16]{0,1:T(8,128)S(1)}, f32[512,512]{1,0:T(8,128)S(1)}) fusion(f32[512,16]{0,1:T(8,128)S(1)} %get-tuple-element.1226, f32[512,512]{1,0:T(8,128)S(1)} %fusion.254, f32[512,16]{0,1:T(8,128)S(1)} %bitcast_bitcast_fusion.7, pred[512,512]{1,0:T(8,128)(4,1)S(1)} %fusion.255, ...), kind=kOutput, calls=%fused_computation.69.clone.1 | convolution fusion | flops 3283853312 | bytes 6717440 | tf_op jit(solution)/shard_map/transpose(jvp())/while/body/eval_jaxpr/checkpoint/ijh,jhp->ihp/dot_general | solution.py:42
  654.6 18.2 fusion.259
  676.3 41.0 %dynamic_update_slice.92 = f32[4,512,16,64]{1,0,3,2:T(4,128)} dynamic-update-slice(f32[4,512,16,64]{1,0,3,2:T(4,128)} %get-tuple-element.1321, f32[1,512,16,64]{1,0,3,2:T(1,128)} %copy.223, s32[]{:T(128)S(6)} %sub.279, s32[]{:T(128)} %constant.145.clone.1..sunk.1, s32[]{:T(128)} %constant.145.clone.1..sunk.1, s32[]{:T(128)} %constant.145.clone.1..sunk.1) | dynamic-update-slice | bytes 4194308 | tf_op jit(solution)/shard_map/transpose(jvp())/while/body/jit(dynamic_update_index_in_dim)/dynamic_update_slice | solution.py:68
  758.5 27.1 %fusion.256 = (f32[512,16]{0,1:T(8,128)S(1)}, f32[512,16]{0,1:T(8,128)S(1)}, f32[512,16]{0,1:T(8,128)S(1)}, f32[512,512]{1,0:T(8,128)S(1)}) fusion(f32[512,16]{0,1:T(8,128)S(1)} %get-tuple-element.1226, f32[512,512]{1,0:T(8,128)S(1)} %fusion.254, f32[512,16]{0,1:T(8,128)S(1)} %bitcast_bitcast_fusion.7, pred[512,512]{1,0:T(8,128)(4,1)S(1)} %fusion.255, ...), kind=kOutput, calls=%fused_computation.69.clone.1 | convolution fusion | flops 3283853312 | bytes 6717440 | tf_op jit(solution)/shard_map/transpose(jvp())/while/body/eval_jaxpr/checkpoint/ijh,jhp->ihp/dot_general | solution.py:42
  804.6 18.4 fusion.259
  826.5 41.0 %dynamic_update_slice.92 = f32[4,512,16,64]{1,0,3,2:T(4,128)} dynamic-update-slice(f32[4,512,16,64]{1,0,3,2:T(4,128)} %get-tuple-element.1321, f32[1,512,16,64]{1,0,3,2:T(1,128)} %copy.223, s32[]{:T(128)S(6)} %sub.279, s32[]{:T(128)} %constant.145.clone.1..sunk.1, s32[]{:T(128)} %constant.145.clone.1..sunk.1, s32[]{:T(128)} %constant.145.clone.1..sunk.1) | dynamic-update-slice | bytes 4194308 | tf_op jit(solution)/shard_map/transpose(jvp())/while/body/jit(dynamic_update_index_in_dim)/dynamic_update_slice | solution.py:68
  908.5 27.3 %fusion.256 = (f32[512,16]{0,1:T(8,128)S(1)}, f32[512,16]{0,1:T(8,128)S(1)}, f32[512,16]{0,1:T(8,128)S(1)}, f32[512,512]{1,0:T(8,128)S(1)}) fusion(f32[512,16]{0,1:T(8,128)S(1)} %get-tuple-element.1226, f32[512,512]{1,0:T(8,128)S(1)} %fusion.254, f32[512,16]{0,1:T(8,128)S(1)} %bitcast_bitcast_fusion.7, pred[512,512]{1,0:T(8,128)(4,1)S(1)} %fusion.255, ...), kind=kOutput, calls=%fused_computation.69.clone.1 | convolution fusion | flops 3283853312 | bytes 6717440 | tf_op jit(solution)/shard_map/transpose(jvp())/while/body/eval_jaxpr/checkpoint/ijh,jhp->ihp/dot_general | solution.py:42
  954.8 18.1 fusion.259
  976.4 41.0 %dynamic_update_slice.92 = f32[4,512,16,64]{1,0,3,2:T(4,128)} dynamic-update-slice(f32[4,512,16,64]{1,0,3,2:T(4,128)} %get-tuple-element.1321, f32[1,512,16,64]{1,0,3,2:T(1,128)} %copy.223, s32[]{:T(128)S(6)} %sub.279, s32[]{:T(128)} %constant.145.clone.1..sunk.1, s32[]{:T(128)} %constant.145.clone.1..sunk.1, s32[]{:T(128)} %constant.145.clone.1..sunk.1) | dynamic-update-slice | bytes 4194308 | tf_op jit(solution)/shard_map/transpose(jvp())/while/body/jit(dynamic_update_index_in_dim)/dynamic_update_slice | solution.py:68
  1058.7 27.1 %fusion.256 = (f32[512,16]{0,1:T(8,128)S(1)}, f32[512,16]{0,1:T(8,128)S(1)}, f32[512,16]{0,1:T(8,128)S(1)}, f32[512,512]{1,0:T(8,128)S(1)}) fusion(f32[512,16]{0,1:T(8,128)S(1)} %get-tuple-element.1226, f32[512,512]{1,0:T(8,128)S(1)} %fusion.254, f32[512,16]{0,1:T(8,128)S(1)} %bitcast_bitcast_fusion.7, pred[512,512]{1,0:T(8,128)(4,1)S(1)} %fusion.255, ...), kind=kOutput, calls=%fused_computation.69.clone.1 | convolution fusion | flops 3283853312 | bytes 6717440 | tf_op jit(solution)/shard_map/transpose(jvp())/while/body/eval_jaxpr/checkpoint/ijh,jhp->ihp/dot_general | solution.py:42
  1104.7 18.2 fusion.259
  1126.4 41.0 %dynamic_update_slice.92 = f32[4,512,16,64]{1,0,3,2:T(4,128)} dynamic-update-slice(f32[4,512,16,64]{1,0,3,2:T(4,128)} %get-tuple-element.1321, f32[1,512,16,64]{1,0,3,2:T(1,128)} %copy.223, s32[]{:T(128)S(6)} %sub.279, s32[]{:T(128)} %constant.145.clone.1..sunk.1, s32[]{:T(128)} %constant.145.clone.1..sunk.1, s32[]{:T(128)} %constant.145.clone.1..sunk.1) | dynamic-update-slice | bytes 4194308 | tf_op jit(solution)/shard_map/transpose(jvp())/while/body/jit(dynamic_update_index_in_dim)/dynamic_update_slice | solution.py:68
  1268.9 16.8 fusion.115
  1328.8 59.1 %all-reduce.28 = (f32[4,1024]{1,0:T(4,128)}, f32[1024]{0:T(1024)}, f32[16]{0:T(128)}, f32[16]{0:T(128)}, f32[16]{0:T(128)}, /*index=5*/f32[1024]{0:T(1024)}) all-reduce(f32[4,1024]{1,0:T(4,128)S(1)} %pad_add_fusion, f32[1024]{0:T(1024)S(1)} %get-tuple-element.814, ...), channel_id=1, replica_groups=mesh['dp'=16,'tensor'=2] {'dp'}, use_global_device_ids=true, to_apply=%region_35.36 | all-reduce | flops 6192 | bytes 49536 | tf_op jit(solution)/shard_map/psum | solution.py:219
  1388.0 32.5 %all-reduce.33.cloned.1.call-done = f32[1024,256]{1,0:T(8,128)} async-done(((f32[1024,256]{1,0:T(8,128)}), f32[1024,256]{1,0:T(8,128)}) %all-reduce.33.cloned.1.call-update) | async-done | bytes 1048592 | tf_op jit(solution)/shard_map/psum | solution.py:232
  1422.6 236.2 %all-reduce.35.cloned.1.call-done = (f32[1024,2064]{0,1:T(8,128)}, f32[1024,1024]{1,0:T(8,128)}) async-done(((f32[1024,2064]{0,1:T(8,128)}, f32[1024,1024]{1,0:T(8,128)}), (f32[1024,2064]{0,1:T(8,128)}, f32[1024,1024]{1,0:T(8,128)})) %all-reduce.35.cloned.1.call-update) | async-done | bytes 12648464 | tf_op jit(solution)/shard_map/psum | solution.py:219
  1679.6 80.3 %reduce-scatter.6.cloned.1.call-done = f32[1024,1024]{1,0:T(8,128)} async-done(((f32[2048,1024]{1,0:T(8,128)}), f32[1024,1024]{1,0:T(8,128)}) %reduce-scatter.6.cloned.1.call-update) | async-done | bytes 4194320 | tf_op jit(solution)/shard_map/reduce_scatter | solution.py:207
  1766.5 40.6 %all-reduce.27 = (f32[1024]{0:T(1024)}, f32[4,256]{1,0:T(4,128)}, f32[256]{0:T(256)}) all-reduce(f32[1024]{0:T(1024)S(1)} %get-tuple-element.816, f32[4,256]{1,0:T(4,128)S(1)} %pad_add_fusion.1, f32[256]{0:T(256)S(1)} %get-tuple-element.818), channel_id=1, replica_groups=mesh['dp'=16,'tensor'=2] {'dp','tensor'}, use_global_device_ids=true, to_apply=%region_28.29 | all-reduce | flops 2304 | bytes 18432 | tf_op jit(solution)/shard_map/psum | solution.py:232
  1807.1 55.9 %reduce-scatter.4.cloned.1.call-done = f32[1024,1024]{1,0:T(8,128)} async-done(((f32[2048,1024]{1,0:T(8,128)}), f32[1024,1024]{1,0:T(8,128)}) %reduce-scatter.4.cloned.1.call-update) | async-done | bytes 4194320 | tf_op jit(solution)/shard_map/reduce_scatter | solution.py:179
  (711 shorter events, 635.7 us)
Async XLA Ops:
  7.2 513.8 %copy-start = (bf16[1024,1024]{1,0:T(8,128)(2,1)S(1)}, bf16[1024,1024]{1,0:T(8,128)(2,1)}, u32[]{:S(2)}) copy-start(bf16[1024,1024]{1,0:T(8,128)(2,1)} %param.40) | copy-start | bytes 6291460
  7.2 67.3 %all-gather.3.cloned.1.call-start = ((), (), s32[]{:S(2)}) async-start(), calls=%async_computation.3 | async-start | bytes 6291456 | tf_op jit(solution)/shard_map/all_gather | solution.py:153
  14.9 506.0 %all-gather.5.cloned.1.call-start = ((), (), s32[]{:S(2)}) async-start(), calls=%async_computation.5 | async-start | bytes 6291456 | tf_op jit(solution)/shard_map/all_gather | solution.py:188
  15.0 141.7 %copy-start.33 = (f32[1,2048]{1,0:T(1,128)}, f32[1,2048]{1,0:T(1,128)S(1)}, u32[]{:S(2)}) copy-start(f32[1,2048]{1,0:T(1,128)S(1)} %convert_element_type.140) | copy-start | bytes 24580
  19.0 1266.8 %reduce-scatter.8.cloned.1.call-start = ((), (), s32[]{:S(2)}) async-start(), calls=%async_computation.7 | async-start | bytes 3145728 | tf_op jit(solution)/shard_map/reduce_scatter | solution.py:203
  19.2 70.8 %copy-start.31 = (bf16[1024,16]{1,0:T(8,128)(2,1)}, bf16[1024,16]{1,0:T(8,128)(2,1)S(1)}, u32[]{:S(2)}) copy-start(bf16[1024,16]{1,0:T(8,128)(2,1)S(1)} %copy.92) | copy-start | bytes 98308
  19.3 91.4 %copy-start.53 = (f32[1,1024]{1,0:T(1,128)}, f32[1,1024]{1,0:T(1,128)S(1)}, u32[]{:S(2)}) copy-start(f32[1,1024]{1,0:T(1,128)S(1)} %get-tuple-element.957) | copy-start | bytes 12292
  19.3 91.4 %copy-start.55 = (f32[1,1024]{1,0:T(1,128)}, f32[1,1024]{1,0:T(1,128)S(1)}, u32[]{:S(2)}) copy-start(f32[1,1024]{1,0:T(1,128)S(1)} %get-tuple-element.960) | copy-start | bytes 12292
  19.3 91.4 %copy-start.57 = (f32[1,1024]{1,0:T(1,128)}, f32[1,1024]{1,0:T(1,128)S(1)}, u32[]{:S(2)}) copy-start(f32[1,1024]{1,0:T(1,128)S(1)} %get-tuple-element.958) | copy-start | bytes 12292
  19.3 91.4 %copy-start.59 = (f32[1,1024]{1,0:T(1,128)}, f32[1,1024]{1,0:T(1,128)S(1)}, u32[]{:S(2)}) copy-start(f32[1,1024]{1,0:T(1,128)S(1)} %get-tuple-element.959) | copy-start | bytes 12292
  20.4 131.4 %copy-start.71 = (f32[1,256]{1,0:T(1,128)}, f32[1,256]{1,0:T(1,128)S(1)}, u32[]{:S(2)}) copy-start(f32[1,256]{1,0:T(1,128)S(1)} %get-tuple-element.966) | copy-start | bytes 3076
  20.4 131.4 %copy-start.73 = (f32[1,256]{1,0:T(1,128)}, f32[1,256]{1,0:T(1,128)S(1)}, u32[]{:S(2)}) copy-start(f32[1,256]{1,0:T(1,128)S(1)} %get-tuple-element.969) | copy-start | bytes 3076
  20.4 131.4 %copy-start.75 = (f32[1,256]{1,0:T(1,128)}, f32[1,256]{1,0:T(1,128)S(1)}, u32[]{:S(2)}) copy-start(f32[1,256]{1,0:T(1,128)S(1)} %get-tuple-element.967) | copy-start | bytes 3076
  20.4 131.4 %copy-start.77 = (f32[1,256]{1,0:T(1,128)}, f32[1,256]{1,0:T(1,128)S(1)}, u32[]{:S(2)}) copy-start(f32[1,256]{1,0:T(1,128)S(1)} %get-tuple-element.968) | copy-start | bytes 3076
  20.5 136.2 %copy-start.82 = (f32[16]{0:T(128)}, f32[16]{0:T(128)S(1)}, u32[]{:S(2)}) copy-start(f32[16]{0:T(128)S(1)} %convert_element_type.144) | copy-start | bytes 196
  20.5 136.2 %copy-start.84 = (f32[16]{0:T(128)}, f32[16]{0:T(128)S(1)}, u32[]{:S(2)}) copy-start(f32[16]{0:T(128)S(1)} %fusion.132) | copy-start | bytes 196
  24.5 126.0 %copy-start.22 = (bf16[1024,256]{1,0:T(8,128)(2,1)}, bf16[1024,256]{1,0:T(8,128)(2,1)S(1)}, u32[]{:S(2)}) copy-start(bf16[1024,256]{1,0:T(8,128)(2,1)S(1)} %constant_dynamic-update-slice_fusion) | copy-start | bytes 1572868
  24.6 127.3 %copy-start.37 = (f32[2048]{0:T(1024)}, f32[2048]{0:T(1024)S(1)}, u32[]{:S(2)}) copy-start(f32[2048]{0:T(1024)S(1)} %get-tuple-element.962) | copy-start | bytes 24580
  24.6 127.3 %copy-start.39 = (f32[2048]{0:T(1024)}, f32[2048]{0:T(1024)S(1)}, u32[]{:S(2)}) copy-start(f32[2048]{0:T(1024)S(1)} %get-tuple-element.961) | copy-start | bytes 24580
  24.6 127.3 %copy-start.41 = (f32[2048]{0:T(1024)}, f32[2048]{0:T(1024)S(1)}, u32[]{:S(2)}) copy-start(f32[2048]{0:T(1024)S(1)} %get-tuple-element.963) | copy-start | bytes 24580
  676.3 47.4 %copy-start.96 = (s32[4]{0:T(128)S(1)}, s32[4]{0:T(128)}, u32[]{:S(2)}) copy-start(s32[4]{0:T(128)} %copy-done.95) | copy-start | bytes 52 | tf_op jit(solution)/shard_map/transpose(jvp())/while
  826.5 47.4 %copy-start.96 = (s32[4]{0:T(128)S(1)}, s32[4]{0:T(128)}, u32[]{:S(2)}) copy-start(s32[4]{0:T(128)} %copy-done.95) | copy-start | bytes 52 | tf_op jit(solution)/shard_map/transpose(jvp())/while
  976.4 47.4 %copy-start.96 = (s32[4]{0:T(128)S(1)}, s32[4]{0:T(128)}, u32[]{:S(2)}) copy-start(s32[4]{0:T(128)} %copy-done.95) | copy-start | bytes 52 | tf_op jit(solution)/shard_map/transpose(jvp())/while
  1241.8 178.7 %all-reduce.33.cloned.1.call-start = ((), (), s32[]{:S(2)}) async-start(), calls=%async_computation.8 | async-start | bytes 2097152 | tf_op jit(solution)/shard_map/psum | solution.py:232
  1289.3 369.5 %all-reduce.35.cloned.1.call-start = ((), (), s32[]{:S(2)}) async-start(), calls=%async_computation.9 | async-start | bytes 25296896 | tf_op jit(solution)/shard_map/psum | solution.py:219
  1300.5 459.4 %reduce-scatter.6.cloned.1.call-start = ((), (), s32[]{:S(2)}) async-start(), calls=%async_computation.6 | async-start | bytes 12582912 | tf_op jit(solution)/shard_map/reduce_scatter | solution.py:207
  1317.5 545.5 %reduce-scatter.4.cloned.1.call-start = ((), (), s32[]{:S(2)}) async-start(), calls=%async_computation.4 | async-start | bytes 12582912 | tf_op jit(solution)/shard_map/reduce_scatter | solution.py:179
  1674.2 85.7 %copy-start.23 = (bf16[1024,256]{1,0:T(8,128)(2,1)S(1)}, bf16[1024,256]{1,0:T(8,128)(2,1)}, u32[]{:S(2)}) copy-start(bf16[1024,256]{1,0:T(8,128)(2,1)} %copy-done.22) | copy-start | bytes 1572868
  1674.2 85.7 %copy-start.47 = (f32[1024]{0:T(1024)S(1)}, f32[1024]{0:T(1024)}, u32[]{:S(2)}) copy-start(f32[1024]{0:T(1024)} %copy-done.46) | copy-start | bytes 12292
  1674.2 85.7 %copy-start.49 = (f32[1024]{0:T(1024)S(1)}, f32[1024]{0:T(1024)}, u32[]{:S(2)}) copy-start(f32[1024]{0:T(1024)} %copy-done.48) | copy-start | bytes 12292
  1679.6 183.4 %copy-start.52 = (f32[1,1024]{1,0:T(1,128)S(1)}, f32[1,1024]{1,0:T(1,128)}, u32[]{:S(2)}) copy-start(f32[1,1024]{1,0:T(1,128)} %copy-done.51) | copy-start | bytes 12292
  1679.6 183.4 %copy-start.70 = (f32[1024]{0:T(1024)S(1)}, f32[1024]{0:T(1024)}, u32[]{:S(2)}) copy-start(f32[1024]{0:T(1024)} %get-tuple-element.964) | copy-start | bytes 12292
  (152 other events, 2529.0 us)
Sparse Core Ops, SparseCore 0:
  15.0 59.4 all-gather.2
  76.6 56.7 all-gather.4
  1241.9 32.1 reduce-scatter.7
  1289.5 130.9 all-reduce.32
  1425.0 233.8 all-reduce.34
  1661.0 98.8 reduce-scatter.5
  1762.2 100.7 reduce-scatter.3
where the time goes:
time: 1900 us; the launch traced here: 1880 us
  local copies, waits for them, and re-layouts  572 us (30%)
  matrix products  499 us (26%)
  waiting for transfers between devices  455 us (24%)
  other arithmetic  207 us (11%)
  blocking collectives  110 us (6%)
  loops' own time  20.6 us (1%)
    dynamic_update_slice x36, local copies, waits for them, and re-layouts, ssd_scan(): lax.scan(jax.checkpoint(block_step), (state_init, jnp.array(-1, jnp.int32...  370 us
    dot_general x12, matrix products, block_step(): inner_part = jnp.einsum('ijh,jhp->ihp', mixing, x_block, precision=highest)  271 us
    psum x1, waiting for transfers between devices, shards(): lax.psum((grad_head_weight, grad_w_out, mixer_grads[3], mixer_grads[4], m...  236 us
    reduce_scatter x1, waiting for transfers between devices, shards(): lax.psum_scatter(contract_cols(head_grad, head_weight), 'tensor', scatter...  80.3 us
    psum x1, blocking collectives, shards(): lax.psum((grad_head_weight, grad_w_out, mixer_grads[3], mixer_grads[4], m...  59.1 us
    reduce_scatter x1, waiting for transfers between devices, shards(): lax.psum_scatter(jnp.dot(normed_gate, w_out, preferred_element_type=jnp.f...  55.9 us
    all_gather x1, waiting for transfers between devices, shards(): normed_all = lax.all_gather(normed_own, 'tensor', axis=0, tiled=True)  49.9 us
    another operation x34, other arithmetic  49.1 us
  transfers between devices with their start and end apart: 7, of which 5 were waited for; matrix products, arithmetic and copies ran while one was open for 30% of the time, Pallas kernels for 0%

commit v1 on v0

v1 whole, which is shorter than its diff:
```python
import functools

import jax
import jax.numpy as jnp
from jax import lax
from jax.experimental import pallas as pl
from jax.experimental.pallas import tpu as pltpu
from jax.sharding import PartitionSpec as P

EPSILON = 1e-05
HEAD = 64
LANES = 128
CHUNK = 128
TAPS = 4
FAR = -1e30
F32 = jnp.float32
BF16 = jnp.bfloat16
HIGHEST = lax.Precision.HIGHEST

LIVE, PREV, NEXT, SCENE, CARRIED, TAIL, KEEP = 0, 1, 4, 7, 8, 9, 10


def nn(left, right):
    return jnp.dot(left, right, preferred_element_type=F32)


def nt(left, right):
    return lax.dot_general(left, right, (((1,), (1,)), ((), ())), preferred_element_type=F32)


def split(value):
    high = value.astype(BF16)
    return high, (value - high.astype(F32)).astype(BF16)


def fine(product, left, right):
    left_high, left_low = split(left)
    right_high, right_low = split(right)
    return product(left_high, right_high) + (product(left_high, right_low) + product(left_low, right_high))


def tn(left, right):
    return lax.dot_general(left, right, (((0,), (0,)), ((), ())), preferred_element_type=F32)


def sigmoid(value):
    return 1.0 / (1.0 + jnp.exp(-value))


def softplus(value):
    small = jnp.exp(-jnp.abs(value))
    shifted = 1.0 + small
    tiny = shifted == 1.0
    ratio = jnp.log(shifted) * small / jnp.where(tiny, 1.0, shifted - 1.0)
    return jnp.maximum(value, 0.0) + jnp.where(tiny, small, ratio)


def spread(rows, table):
    high, low = split(rows)
    return nn(high, table) + nn(low, table)


def fold8(value):
    return jnp.sum(value.reshape(value.shape[0] // 8, 8, value.shape[1]), axis=0)


def head_pair(value):
    lane = lax.broadcasted_iota(jnp.int32, value.shape, 1)
    zero = jnp.zeros_like(value)
    return jnp.concatenate(
        [jnp.where(lane < HEAD, value, zero), jnp.where(lane < HEAD, zero, value)], axis=0
    )


def forward_kernel(
    per_block, at_ref, mine_ref, other_ref, zmine_ref, zother_ref, col_ref, row_ref, kx_ref, kbc_ref, hp_ref, ex_ref,
    gated_ref, silu_ref, slope_ref, xc_ref, sp_ref, raw_ref, bc_ref, spbc_ref, dt_ref, cum_ref, ds_ref, sq_ref, st_ref,
    xs, gs, state,
):
    rows, width = xc_ref.shape
    double = bc_ref.shape[1]
    count = double // 2
    own = pl.program_id(0) // per_block == at_ref[0]

    @pl.when(pl.program_id(0) == 0)
    def _():
        xs[0:8, :] = jnp.zeros((8, xs.shape[1]), F32)
        state[...] = jnp.zeros_like(state)

    @pl.when(own)
    def _():
        xs[8:, :] = mine_ref[...]
        gs[...] = zmine_ref[...]

    @pl.when(jnp.logical_not(own))
    def _():
        xs[8:, :] = other_ref[...]
        gs[...] = zother_ref[...]

    raw_ref[...] = xs[8:, : width + double].astype(BF16)
    live = col_ref[:, LIVE : LIVE + 1]
    same = [col_ref[:, PREV + lag : PREV + lag + 1] for lag in range(TAPS - 1)]

    side = slice(width, width + double)
    raw = xs[8:, side]
    pre = kbc_ref[TAPS : TAPS + 1, :] + kbc_ref[TAPS - 1 : TAPS, :] * raw
    for lag in range(1, TAPS):
        tap = kbc_ref[TAPS - 1 - lag : TAPS - lag, :]
        pre = pre + tap * (xs[8 - lag : 8 - lag + rows, side] * same[lag - 1])
    sig = sigmoid(pre)
    act = pre * sig
    spbc_ref[...] = (sig * (1.0 + pre * (1.0 - sig))).astype(spbc_ref.dtype)
    bc_ref[...] = act
    act16 = act.astype(BF16)
    b16 = act16[:, :count]
    c16 = act16[:, count:]

    biased = xs[8:, width + double :] + hp_ref[0:1, :]
    ds_ref[...] = sigmoid(biased) * live
    step = softplus(biased) * live
    dt_ref[...] = step
    decay = step * hp_ref[1:2, :]
    above = lax.broadcasted_iota(jnp.int32, (rows, rows), 0)
    along = lax.broadcasted_iota(jnp.int32, (rows, rows), 1)
    lower = above >= along
    cum = jnp.dot(lower.astype(F32), decay, precision=HIGHEST, preferred_element_type=F32)
    cum_ref[...] = cum
    cum_t = cum.T
    last = cum[rows - 1 : rows, :]
    from_start = jnp.exp(cum) * col_ref[:, CARRIED : CARRIED + 1]
    to_end = jnp.exp(last - cum) * col_ref[:, TAIL : TAIL + 1]
    keep = jnp.exp(last) * col_ref[0:1, KEEP : KEEP + 1]
    table = ex_ref[...]
    wide = spread(jnp.concatenate([step, from_start, to_end, jnp.broadcast_to(keep, (8, LANES))], axis=0), table)

    mask = lower & (col_ref[:, SCENE : SCENE + 1] == row_ref[0:1, :])
    scores = nt(c16, b16)
    b_t = act[:, :count].T
    squares = jnp.zeros((rows, LANES), F32)
    for group in range(width // LANES):
        part = slice(group * LANES, (group + 1) * LANES)
        pre = kx_ref[TAPS : TAPS + 1, part] + kx_ref[TAPS - 1 : TAPS, part] * xs[8:, part]
        for lag in range(1, TAPS):
            tap = kx_ref[TAPS - 1 - lag : TAPS - lag, part]
            pre = pre + tap * (xs[8 - lag : 8 - lag + rows, part] * same[lag - 1])
        sig = sigmoid(pre)
        xc = pre * sig * live
        xc_ref[:, part] = xc
        sp_ref[:, part] = (sig * (1.0 + pre * (1.0 - sig)) * live).astype(BF16)
        both = []
        for head in (2 * group, 2 * group + 1):
            gap = cum[:, head : head + 1] - cum_t[head : head + 1, :]
            weight = jnp.exp(jnp.where(mask, gap, FAR))
            both.append((weight * scores).astype(BF16))
        stepped = xc * wide[:rows, part]
        inner = nn(jnp.concatenate(both, axis=1), head_pair(stepped.astype(BF16)))
        old = state[:, part]
        old16 = old.astype(BF16)
        st_ref[0, :, part] = old
        mixed = inner + nn(c16, old16) * wide[rows : 2 * rows, part] + kx_ref[TAPS + 1 : TAPS + 2, part] * xc
        fed = stepped * wide[2 * rows : 3 * rows, part]
        state[:, part] = old * wide[3 * rows : 3 * rows + 1, part] + fine(nn, b_t, fed)
        gate = gs[:, part]
        sig = sigmoid(gate)
        silu = gate * sig
        gated = mixed * silu
        gated_ref[:, part] = (gated * kx_ref[TAPS + 2 : TAPS + 3, part]).astype(BF16)
        silu_ref[:, part] = silu.astype(BF16)
        slope_ref[:, part] = (mixed * sig * (1.0 + gate * (1.0 - sig))).astype(BF16)
        squares = squares + gated * gated
    sq_ref[...] = nt(jnp.ones((8, LANES), BF16), squares.astype(BF16))
    xs[0:8, :] = xs[rows : rows + 8, :]


def backward_kernel(
    at_ref, dy_ref, xc_ref, sp_ref, x_ref, bc_ref, spbc_ref, dt_ref, cum_ref, ds_ref, col_ref, row_ref,
    st_ref, kx_ref, kbc_ref, hp_ref, ex_ref, fo_ref,
    out_ref, gk_ref, gkbc_ref, gh_ref,
    dvs, dbs, grad, rowsum,
):
    rows, width = xc_ref.shape
    double = bc_ref.shape[1]
    count = double // 2

    @pl.when(pl.program_id(0) == 0)
    def _():
        dvs[rows:, :] = jnp.zeros((8, width), F32)
        dbs[rows:, :] = jnp.zeros((8, double), F32)
        grad[...] = jnp.zeros_like(grad)
        rowsum[...] = jnp.zeros_like(rowsum)
        gk_ref[...] = jnp.zeros_like(gk_ref)
        gkbc_ref[...] = jnp.zeros_like(gkbc_ref)
        gh_ref[...] = jnp.zeros_like(gh_ref)

    @pl.when(pl.program_id(0) > 0)
    def _():
        dvs[rows:, :] = dvs[0:8, :]
        dbs[rows:, :] = dbs[0:8, :]

    same = [col_ref[:, NEXT + lag : NEXT + lag + 1] for lag in range(TAPS - 1)]
    b = bc_ref[:, :count]
    c = bc_ref[:, count:]
    step = dt_ref[...]
    cum = cum_ref[...]
    cum_t = cum.T
    last = cum[rows - 1 : rows, :]
    from_start = jnp.exp(cum) * col_ref[:, CARRIED : CARRIED + 1]
    to_end = jnp.exp(last - cum) * col_ref[:, TAIL : TAIL + 1]
    keep = jnp.exp(last) * col_ref[0:1, KEEP : KEEP + 1]
    table = ex_ref[...]
    wide = spread(jnp.concatenate([step, from_start, to_end, jnp.broadcast_to(keep, (8, LANES))], axis=0), table)

    above = lax.broadcasted_iota(jnp.int32, (rows, rows), 0)
    along = lax.broadcasted_iota(jnp.int32, (rows, rows), 1)
    upper = above <= along
    mask = upper & (col_ref[:, SCENE : SCENE + 1] == row_ref[0:1, :])
    scores = fine(nt, b, c)
    c_t = c.T
    lane = lax.broadcasted_iota(jnp.int32, (rows, LANES), 1)

    d_scores = jnp.zeros((rows, rows), F32)
    d_b = jnp.zeros((rows, count), F32)
    d_c = jnp.zeros((rows, count), F32)
    d_cum = jnp.zeros((rows, LANES), F32)
    d_step = jnp.zeros((rows, LANES), F32)
    d_last = jnp.zeros((8, LANES), F32)
    for group in range(width // LANES):
        part = slice(group * LANES, (group + 1) * LANES)
        dy = dy_ref[:, part]
        xc = xc_ref[:, part]
        wide_step = wide[:rows, part]
        wide_end = wide[2 * rows : 3 * rows, part]
        fold = fo_ref[part, :]
        pair = head_pair(dy)
        stepped = xc * wide_step
        back = fine(nt, stepped, pair)
        both = []
        for which, head in enumerate((2 * group, 2 * group + 1)):
            gap = cum_t[head : head + 1, :] - cum[:, head : head + 1]
            weight = jnp.exp(jnp.where(mask, gap, FAR))
            both.append(weight * scores)
            weighted = back[:, which * rows : (which + 1) * rows] * weight
            d_scores = d_scores + weighted
            inner = weighted * scores
            rowsum[head : head + 1, :] = jnp.sum(inner, axis=0, keepdims=True)
            d_cum = d_cum - jnp.where(lane == head, jnp.sum(inner, axis=1, keepdims=True), 0.0)
        d_stepped = fine(nn, jnp.concatenate(both, axis=1), pair)
        old = st_ref[0, :, part]
        after = grad[:, part]
        carried = dy * wide[rows : 2 * rows, part]
        fed = stepped * wide_end
        from_after = fine(nn, b, after)
        to_last = fed * from_after
        d_b = d_b + fine(nt, fed, after)
        d_c = d_c + fine(nt, carried, old)
        d_cum = d_cum + spread(carried * fine(nn, c, old) - to_last, fold)
        kept = wide[3 * rows : 3 * rows + 1, part]
        total = fold8(to_last) + fold8(after * old) * kept
        d_last = d_last + spread(total, fold)
        grad[:, part] = after * kept + fine(nn, c_t, carried)
        d_stepped = d_stepped + from_after * wide_end
        d_xc = d_stepped * wide_step + kx_ref[TAPS + 1 : TAPS + 2, part] * dy
        d_step = d_step + spread(d_stepped * xc, fold)
        dv = d_xc * sp_ref[:, part].astype(F32)
        dvs[0:rows, part] = dv
        x = x_ref[:, part].astype(F32)
        xg = kx_ref[TAPS - 1 : TAPS, part] * dv
        gk_ref[8 * (TAPS - 1) : 8 * TAPS, part] += fold8(x * dv)
        gk_ref[8 * TAPS : 8 * TAPS + 8, part] += fold8(dv)
        gk_ref[8 * TAPS + 8 : 8 * TAPS + 16, part] += fold8(dy * xc)
        for lag in range(1, TAPS):
            moved = dvs[lag : lag + rows, part] * same[lag - 1]
            xg = xg + kx_ref[TAPS - 1 - lag : TAPS - lag, part] * moved
            gk_ref[8 * (TAPS - 1 - lag) : 8 * (TAPS - lag), part] += fold8(x * moved)
        out_ref[:, part] = xg.astype(BF16)

    d_b = d_b + fine(nn, d_scores, c)
    d_c = d_c + fine(nn, d_scores.T, b)
    for side, value in ((0, d_b), (1, d_c)):
        part = slice(side * count, (side + 1) * count)
        dv = value * spbc_ref[:, part].astype(F32)
        dbs[0:rows, part] = dv
        raw = x_ref[:, width + side * count : width + (side + 1) * count].astype(F32)
        out = kbc_ref[TAPS - 1 : TAPS, part] * dv
        gkbc_ref[8 * (TAPS - 1) : 8 * TAPS, part] += fold8(raw * dv)
        gkbc_ref[8 * TAPS : 8 * TAPS + 8, part] += fold8(dv)
        for lag in range(1, TAPS):
            moved = dbs[lag : lag + rows, part] * same[lag - 1]
            out = out + kbc_ref[TAPS - 1 - lag : TAPS - lag, part] * moved
            gkbc_ref[8 * (TAPS - 1 - lag) : 8 * (TAPS - lag), part] += fold8(raw * moved)
        out_ref[:, width + side * count : width + (side + 1) * count] = out.astype(BF16)

    d_cum = d_cum + rowsum[...].T
    d_decay = jnp.dot(upper.astype(F32), d_cum, precision=HIGHEST, preferred_element_type=F32)
    d_decay = d_decay + jnp.sum(d_last, axis=0, keepdims=True)
    d_step = d_step + d_decay * hp_ref[1:2, :]
    d_raw = d_step * ds_ref[...]
    gh_ref[0:8, :] += fold8(d_raw)
    gh_ref[8:16, :] += fold8(d_decay * step * hp_ref[1:2, :])
    out_ref[:, width + double :] = d_raw.astype(BF16)


def physical(step, at, size, per_block):
    return lax.rem(at - step // per_block + size, size) * per_block + lax.rem(step, per_block)


def call_forward(at, size, mine, other, zmine, zother, col, row, kx, kbc, hp, expand):
    cat = mine.shape[1]
    width = zmine.shape[1]
    double = cat - width - LANES
    total = mine.shape[0] * size
    steps = total // CHUNK
    per_block = mine.shape[0] // CHUNK

    def own_place(i, at_ref):
        return jnp.clip(i - at_ref[0] * per_block, 0, per_block - 1), 0

    def other_place(i, at_ref):
        place = physical(i, at_ref[0], size, per_block) - per_block
        resting = jnp.where(at_ref[0] == 0, (size - 2) * per_block, per_block - 1)
        return jnp.where(place < 0, resting, place), 0

    def rows(cols):
        return pl.BlockSpec((CHUNK, cols), lambda i, at_ref: (i, 0))

    def moved(cols):
        return pl.BlockSpec((CHUNK, cols), lambda i, at_ref: (physical(i, at_ref[0], size, per_block), 0))

    def whole(array):
        return pl.BlockSpec(array.shape, lambda i, at_ref: (0, 0))

    lanes8 = pl.BlockSpec((8, CHUNK), lambda i, at_ref: (0, i))
    shape = jax.ShapeDtypeStruct
    return pl.pallas_call(
        functools.partial(forward_kernel, per_block),
        grid_spec=pltpu.PrefetchScalarGridSpec(
            num_scalar_prefetch=1,
            grid=(steps,),
            in_specs=[
                pl.BlockSpec((CHUNK, cat), own_place), pl.BlockSpec((CHUNK, cat), other_place),
                pl.BlockSpec((CHUNK, width), own_place), pl.BlockSpec((CHUNK, width), other_place),
                rows(LANES), lanes8, whole(kx), whole(kbc), whole(hp), whole(expand),
            ],
            out_specs=[
                moved(width), moved(width), moved(width), rows(width), rows(width), rows(width + double),
                rows(double), rows(double), rows(LANES), rows(LANES), rows(LANES), lanes8,
                pl.BlockSpec((1, double // 2, width), lambda i, at_ref: (i, 0, 0)),
            ],
            scratch_shapes=[
                pltpu.VMEM((CHUNK + 8, cat), F32),
                pltpu.VMEM((CHUNK, width), F32),
                pltpu.VMEM((double // 2, width), F32),
            ],
        ),
        out_shape=[
            shape((total, width), BF16), shape((total, width), BF16), shape((total, width), BF16),
            shape((total, width), F32), shape((total, width), BF16), shape((total, width + double), BF16),
            shape((total, double), F32), shape((total, double), BF16),
            shape((total, LANES), F32), shape((total, LANES), F32), shape((total, LANES), F32), shape((8, total), F32),
            shape((steps, double // 2, width), F32),
        ],
        name="scan_forward",
    )(at, mine, other, zmine, zother, col, row, kx, kbc, hp, expand)


def call_backward(at, size, dy, xc, sp, raw, bc, spbc, step, cum, dsig, col, row, states, kx, kbc, hp, expand, fold):
    total, width = xc.shape
    double = bc.shape[1]
    cat = width + double + LANES
    steps = total // CHUNK
    per_block = steps // size

    def rows(cols):
        return pl.BlockSpec((CHUNK, cols), lambda i, at_ref: (steps - 1 - i, 0))

    def moved(cols):
        return pl.BlockSpec((CHUNK, cols), lambda i, at_ref: (physical(steps - 1 - i, at_ref[0], size, per_block), 0))

    def whole(array):
        return pl.BlockSpec(array.shape, lambda i, at_ref: (0, 0))

    lanes8 = pl.BlockSpec((8, CHUNK), lambda i, at_ref: (0, steps - 1 - i))
    shape = jax.ShapeDtypeStruct
    sums = [shape((8 * (TAPS + 2), width), F32), shape((8 * (TAPS + 1), double), F32), shape((16, LANES), F32)]
    return pl.pallas_call(
        backward_kernel,
        grid_spec=pltpu.PrefetchScalarGridSpec(
            num_scalar_prefetch=1,
            grid=(steps,),
            in_specs=[
                moved(width), rows(width), rows(width), rows(width + double),
                rows(double), rows(double), rows(LANES), rows(LANES), rows(LANES), rows(LANES), lanes8,
                pl.BlockSpec((1, double // 2, width), lambda i, at_ref: (steps - 1 - i, 0, 0)),
                whole(kx), whole(kbc), whole(hp), whole(expand), whole(fold),
            ],
            out_specs=[moved(cat)] + [whole(member) for member in sums],
            scratch_shapes=[
                pltpu.VMEM((CHUNK + 8, width), F32),
                pltpu.VMEM((CHUNK + 8, double), F32),
                pltpu.VMEM((double // 2, width), F32),
                pltpu.VMEM((LANES, CHUNK), F32),
            ],
        ),
        out_shape=[shape((total, cat), BF16)] + sums,
        name="scan_backward",
    )(at, dy, xc, sp, raw, bc, spbc, step, cum, dsig, col, row, states, kx, kbc, hp, expand, fold)


def row_tables(scene, live):
    total = scene.shape[0]
    far = jnp.full((TAPS - 1,), -1, scene.dtype)
    before = jnp.concatenate([far, scene])
    after = jnp.concatenate([scene, far])
    lines = [live]
    lines += [(before[TAPS - 1 - lag : TAPS - 1 - lag + total] == scene).astype(F32) for lag in range(1, TAPS)]
    lines += [(after[lag : lag + total] == scene).astype(F32) for lag in range(1, TAPS)]
    lines.append(scene.astype(F32))
    blocks = scene.reshape(total // CHUNK, CHUNK)
    last = blocks[:, -1:]
    ahead = jnp.concatenate([jnp.full((1, 1), -1, scene.dtype), last[:-1]])
    lines.append((blocks == ahead).astype(F32).reshape(total))
    lines.append((blocks == last).astype(F32).reshape(total))
    lines.append(jnp.broadcast_to((last == ahead).astype(F32), blocks.shape).reshape(total))
    table = jnp.stack(lines + [jnp.zeros((total,), F32)] * (16 - len(lines)))
    col = jnp.pad(table.T, ((0, 0), (0, LANES - 16)))
    row = jnp.broadcast_to(scene.astype(F32)[None, :], (8, total))
    return col, row


def head_tables(width):
    heads = lax.broadcasted_iota(jnp.int32, (LANES, width), 0)
    owner = lax.broadcasted_iota(jnp.int32, (LANES, width), 1) // HEAD
    expand = (heads == owner).astype(BF16)
    return expand, expand.T


def lane_row(vector):
    return jnp.pad(vector, (0, LANES - vector.shape[0]))


def swap(value, axis, size, bit):
    return lax.ppermute(value, axis, [(place, place ^ bit) for place in range(size)])


def bits(size):
    return [1 << power for power in range(size.bit_length() - 1)]


def sum_small(value, axes):
    for axis in axes:
        size = lax.axis_size(axis)
        for bit in bits(size):
            value = value + swap(value, axis, size, bit)
    return value


def sum_large(values, axis, middle):
    size = lax.axis_size(axis)
    place = lax.axis_index(axis)
    kinds = (BF16, F32)
    for bit in bits(size):
        upper = (place & bit) > 0
        halves = []
        for value, kind in zip(values, kinds):
            half = value.shape[0] // 2
            low, high = value[:half], value[half:]
            other = swap(jnp.where(upper, low, high).astype(kind), axis, size, bit)
            halves.append(jnp.where(upper, high, low) + other.astype(F32))
        values = halves
    values = [value.astype(BF16) for value in middle(values)]
    for bit in reversed(bits(size)):
        upper = (place & bit) > 0
        others = [swap(value, axis, size, bit) for value in values]
        values = [
            jnp.concatenate([jnp.where(upper, other, value), jnp.where(upper, value, other)])
            for value, other in zip(values, others)
        ]
    return [value.astype(F32) for value in values]


def shards(
    tokens, scene_ids, valid, norm_gain, w_z, w_x, w_b, w_c, w_dt, conv_x, conv_x_bias, conv_bc, conv_bc_bias,
    dt_bias, a_log, d_skip, gate_gain, w_out, cotangent,
):
    size = lax.axis_size("tensor")
    index = lax.axis_index("tensor")
    rows_own, model_width = tokens.shape
    width = w_z.shape[1]
    heads = w_dt.shape[1]
    double = 2 * w_b.shape[1]
    inner_width = width * size
    scene = scene_ids[0]
    live = valid[0].astype(F32)

    def reorder(value):
        blocks = [
            lax.dynamic_slice_in_dim(value, lax.rem(index + size - block, size) * rows_own, rows_own)
            for block in range(size)
        ]
        return jnp.concatenate(blocks)

    def rotate(value):
        return [
            lax.ppermute(value, "tensor", [(source, (source + shift) % size) for source in range(size)])
            for shift in range(1, size)
        ]

    def scatter(value):
        total = value[:rows_own].astype(F32)
        for shift in range(1, size):
            part = value[(size - shift) * rows_own : (size - shift + 1) * rows_own].astype(BF16)
            pairs = [(source, (source + shift) % size) for source in range(size)]
            total = total + lax.ppermute(part, "tensor", pairs).astype(F32)
        return total

    others = rotate(tokens)

    live_first = reorder(live)[:, None]
    live_own = live_first[:rows_own]
    col, row = row_tables(scene, live)
    expand, fold = head_tables(width)
    gain_in = norm_gain.astype(F32)[None, :]
    at = jnp.reshape(index, (1,)).astype(jnp.int32)

    def normalize(value):
        value = value.astype(F32)
        inverse = lax.rsqrt(jnp.mean(value * value, axis=1, keepdims=True) + EPSILON)
        return (value * inverse * gain_in).astype(BF16)

    w_cat = jnp.concatenate([w_x, w_b, w_c, jnp.pad(w_dt, ((0, 0), (0, LANES - heads)))], axis=1)
    normed_own = normalize(tokens)
    mine = nn(normed_own, w_cat)
    zmine = nn(normed_own, w_z)
    cot_own = cotangent * live_own.astype(BF16)
    back_own = nt(cot_own, w_out)
    mine, zmine, back_own, others, held = lax.optimization_barrier((mine, zmine, back_own, others, cotangent))
    cot_others = rotate(held)
    normed_other = normalize(jnp.concatenate(others))
    other = nn(normed_other, w_cat)
    zother = nn(normed_other, w_z)

    skip = jnp.repeat(d_skip.astype(F32), HEAD)
    gain_gate = gate_gain.astype(F32)[None, :]
    kx = jnp.concatenate(
        [conv_x.astype(F32), conv_x_bias.astype(F32)[None], skip[None], gain_gate, jnp.zeros((1, width), F32)]
    )
    kbc = jnp.concatenate([conv_bc.astype(F32), conv_bc_bias.astype(F32)[None], jnp.zeros((3, double), F32)])
    rate = -jnp.exp(a_log.astype(F32))
    hp = jnp.concatenate([lane_row(dt_bias.astype(F32))[None], lane_row(rate)[None], jnp.zeros((6, LANES), F32)])

    gated, silu, slope, xc, sp, raw, bc, spbc, step, cum, dsig, squares, states = call_forward(
        at, size, mine, other, zmine, zother, col, row, kx, kbc, hp, expand
    )
    cot_rest = jnp.concatenate(cot_others) * live_first[rows_own:].astype(BF16)
    cot_all = jnp.concatenate([cot_own, cot_rest])
    normed_grad = jnp.concatenate([back_own, nt(cot_rest, w_out)])
    gated32 = gated.astype(F32)
    dots = jnp.sum(normed_grad * gated32, axis=1)
    stats = sum_small(jnp.stack([squares[0], reorder(dots)]), ["tensor"])
    branch = nn(gated, w_out)
    inverse = reorder(lax.rsqrt(stats[0] / inner_width + EPSILON))[:, None]
    lean = inverse**3 * (reorder(stats[1]) / inner_width)[:, None]

    block_out = (tokens.astype(F32) + live_own * inverse[:rows_own] * scatter(branch)).astype(BF16)
    grad_w_out = tn(gated, (cot_all.astype(F32) * inverse).astype(BF16))

    grad_gate_gain = jnp.sum(normed_grad * gated32 * inverse, axis=0) / gain_gate[0]
    gated_grad = normed_grad * gain_gate * inverse - gated32 * lean / gain_gate
    dy = gated_grad * silu.astype(F32)
    gate_grad = (gated_grad * slope.astype(F32)).astype(BF16)
    normed = jnp.concatenate([normed_own, normed_other])
    grad_w_z = tn(normed, gate_grad)
    early = (grad_w_out.astype(BF16), grad_w_z.astype(BF16))
    early, dy = lax.optimization_barrier((early, dy))
    early = lax.psum(early, "dp")

    cat_grad, gk, gkbc, gh = call_backward(
        at, size, dy, xc, sp, raw, bc, spbc, step, cum, dsig, col, row, states, kx, kbc, hp, expand, fold
    )
    grad_cat = lax.optimization_barrier(tn(normed, cat_grad))

    def shared_columns(values):
        part = values[1][:, :double]
        for bit in bits(size):
            part = part + swap(part, "tensor", size, bit)
        return [values[0], jnp.concatenate([part, values[1][:, double:]], axis=1)]

    late, rest = sum_large([grad_cat[:, :width], grad_cat[:, width:]], "dp", shared_columns)
    back = nt(gate_grad, w_z) + nt(cat_grad, w_cat)
    normed_in_grad = scatter(back)

    weighted = grad_cat * w_cat.astype(F32)
    norm_part = jnp.sum(weighted, axis=1) + jnp.sum(grad_w_z * w_z.astype(F32), axis=1)
    gk = gk.reshape(TAPS + 2, 8, width).sum(1)
    gkbc = gkbc.reshape(TAPS + 1, 8, double).sum(1)
    gh = gh.reshape(2, 8, LANES).sum(1)
    g_skip = gk[TAPS + 1].reshape(heads, HEAD).sum(1)
    local = jnp.concatenate([gk[: TAPS + 1].reshape(-1), grad_gate_gain, gh.reshape(-1), lane_row(g_skip)])
    shared = jnp.concatenate([norm_part / norm_gain.astype(F32), gkbc.reshape(-1)])
    cut = local.shape[0]
    small = jnp.concatenate([local, shared])
    small = jnp.pad(small, (0, -small.shape[0] % 1024)).reshape(-1, LANES)
    small = sum_small(small, ["dp"]).reshape(-1)
    local = small[:cut]
    shared = sum_small(small[cut:].reshape(-1, LANES), ["tensor"]).reshape(-1)
    taps = local[: (TAPS + 1) * width].reshape(TAPS + 1, width)
    local = local[(TAPS + 1) * width :]
    taps_bc = shared[model_width : model_width + (TAPS + 1) * double].reshape(TAPS + 1, double)

    resid = tokens.astype(F32)
    inverse_in = lax.rsqrt(jnp.mean(resid * resid, axis=1, keepdims=True) + EPSILON)
    inner = jnp.sum(gain_in * normed_in_grad * resid, axis=1, keepdims=True)
    grad_tokens = (
        cotangent.astype(F32)
        + inverse_in * gain_in * normed_in_grad
        - resid * inverse_in**3 * (inner / model_width)
    ).astype(BF16)
    return (
        block_out,
        grad_tokens,
        shared[:model_width],
        early[1].astype(F32),
        late,
        rest[:, : double // 2],
        rest[:, double // 2 : double],
        rest[:, double : double + heads],
        taps[:TAPS],
        taps[TAPS],
        taps_bc[:TAPS],
        taps_bc[TAPS],
        local[width : width + heads],
        local[width + LANES : width + LANES + heads],
        local[width + 2 * LANES : width + 2 * LANES + heads],
        local[:width],
        early[0].astype(F32),
    )


def solution(mesh):
    own = P(("dp", "tensor"), None)
    packs, both = P("dp", None), P()
    cols, vector = P(None, "tensor"), P("tensor")
    in_specs = (
        own, packs, packs, both, cols, cols, both, both, cols, cols, vector, both, both,
        vector, vector, vector, vector, P("tensor", None), own,
    )
    out_specs = (
        own, own, both, cols, cols, both, both, cols, cols, vector, both, both,
        vector, vector, vector, vector, P("tensor", None),
    )
    return jax.shard_map(shards, mesh=mesh, in_specs=in_specs, out_specs=out_specs, check_vma=False)
```

time: 1900 us -> 452 us (0.24)
  local copies, waits for them, and re-layouts: 572 us -> 32.2 us
  matrix products: 499 us -> 85.3 us
  waiting for transfers between devices: 455 us -> 86.9 us
  other arithmetic: 207 us -> 66.4 us
  Pallas kernels: 0 us -> 118 us
  blocking collectives: 110 us -> 0 us
  starting transfers between devices: 0.29 us -> 38.3 us
  loops' own time: 20.6 us -> 0 us
    dot_general x57 -> x12, matrix products: 466 us -> 85.3 us  [the longest x3 29.1 us: tn(): lax.dot_general(left, right, (((0,), (0,)), ((), ())), preferred_element_...]
    dynamic_update_slice x36 -> x0, local copies, waits for them, and re-layouts: 370 us -> none  [ssd_scan(): lax.scan(jax.checkpoint(block_step), (state_init, jnp.array(-1, jnp.int32...]
    psum x2 -> x1, waiting for transfers between devices: 269 us -> 0.01 us  [shards(): early = lax.psum(early, 'dp')]
    reduce_scatter x3 -> x0, waiting for transfers between devices: 136 us -> none  [the longest x1 80.3 us: shards(): lax.psum_scatter(contract_cols(head_grad, head_weight), 'tensor', scatter...]
    pallas_call x0 -> x2, Pallas kernels: none -> 118 us  [the longest x1 79.8 us: call_backward(): pl.pallas_call(backward_kernel, grid_spec=pltpu.PrefetchScalarGridSpec(nu...]
    psum x4 -> x0, blocking collectives: 110 us -> none  [the longest x1 59.1 us: shards(): lax.psum((grad_head_weight, grad_w_out, mixer_grads[3], mixer_grads[4], m...]
    ppermute x0 -> x27, waiting for transfers between devices: none -> 86.8 us  [the longest x23 86.8 us: swap(): lax.ppermute(value, axis, [(place, place ^ bit) for place in range(size)])]
    another operation x38 -> x3, other arithmetic: 52.4 us -> 1.07 us  [the longest x1 1.04 us: row_tables(): table = jnp.stack(lines + [jnp.zeros((total,), F32)] * (16 - len(lines)))]
  transfers between devices with their start and end apart: 7 -> 28, of which waited for: 5 -> 15; matrix products, arithmetic and copies ran while one was open for 30% -> 38% of each run, Pallas kernels for 0% -> 27%
where the time goes in v1:
time: 452 us; the launch traced here: 443 us
  Pallas kernels  118 us (26%)
  waiting for transfers between devices  86.9 us (19%)
  matrix products  85.3 us (19%)
  other arithmetic  66.4 us (15%)
  starting transfers between devices  38.3 us (8%)
  local copies, waits for them, and re-layouts  32.2 us (7%)
  between operations  15.5 us (3%)
    ppermute x23, waiting for transfers between devices, swap(): lax.ppermute(value, axis, [(place, place ^ bit) for place in range(size)])  86.8 us
    pallas_call x1, Pallas kernels, call_backward(): pl.pallas_call(backward_kernel, grid_spec=pltpu.PrefetchScalarGridSpec(nu...  79.8 us
    pallas_call x1, Pallas kernels, call_forward(): pl.pallas_call(functools.partial(forward_kernel, per_block), grid_spec=pl...  38.2 us
    ppermute x23, starting transfers between devices, swap(): lax.ppermute(value, axis, [(place, place ^ bit) for place in range(size)])  34.4 us
    dot_general x3, matrix products, tn(): lax.dot_general(left, right, (((0,), (0,)), ((), ())), preferred_element_...  29.1 us
    dot_general x4, matrix products, nt(): lax.dot_general(left, right, (((1,), (1,)), ((), ())), preferred_element_...  28.8 us
    dot_general x5, matrix products, nn(): return jnp.dot(left, right, preferred_element_type=F32)  27.4 us
    unnamed x93, local copies, waits for them, and re-layouts  17.1 us
  transfers between devices with their start and end apart: 28, of which 15 were waited for; matrix products, arithmetic and copies ran while one was open for 38% of the time, Pallas kernels for 27%

profile of v1, /device:TPU:0, one launch (start us, length us, event | category | flops | bytes accessed | tf_op | source)
XLA Modules:
  0.0 442.6 jit_solution(2220179901726933496)
XLA Ops:
  30.0 4.0 copy.84
  34.0 3.2 broadcast_multiply_fusion.1
  41.1 6.7 %fusion.65.zmine_ref = f32[1024,1024]{1,0:T(8,128)} fusion(bf16[1024,1024]{1,0:T(8,128)(2,1)} %fusion.9, bf16[1024,1024]{1,0:T(8,128)(2,1)} %param.23), kind=kOutput, calls=%fused_computation.182 | convolution fusion | flops 2147483648 | bytes 8388608 | tf_op jit(solution)/shard_map/dot_general | solution.py:24
  47.8 4.4 fusion.66
  52.2 5.7 %fusion.56.mine_ref = f32[1024,1408]{1,0:T(8,128)} fusion(bf16[1024,1024]{1,0:T(8,128)(2,1)S(1)} %copy-done.13, bf16[1024,16]{1,0:T(8,128)(2,1)S(1)} %copy.78, bf16[1024,128]{1,0:T(8,128)(2,1)S(1)} %copy-done.21, bf16[1024,128]{1,0:T(8,128)(2,1)S(1)} %copy-done.24, bf16[1024,1024]{1,0:T(8,128)(2,1)S(1)} %copy-done.18), kind=kOutput, calls=%fused_computation.176 | convolution fusion | flops 2967207936 | bytes 10518528 | tf_op jit(solution)/shard_map/dot_general | solution.py:24
  62.4 4.4 fusion.67.zother_ref
  66.7 6.2 %fusion.54.other_ref = f32[1024,1408]{1,0:T(8,128)} fusion(bf16[1024,1024]{1,0:T(8,128)(2,1)S(1)} %fusion.6, bf16[1024,16]{1,0:T(8,128)(2,1)S(1)} %copy.78, bf16[1024,128]{1,0:T(8,128)(2,1)S(1)} %copy-done.21, bf16[1024,128]{1,0:T(8,128)(2,1)S(1)} %copy-done.24, bf16[1024,1024]{1,0:T(8,128)(2,1)S(1)} %copy-done.18), kind=kOutput, calls=%fused_computation.175 | convolution fusion | flops 2967207936 | bytes 10518528 | tf_op jit(solution)/shard_map/dot_general | solution.py:24
  73.5 38.2 %scan_forward.1 = (bf16[2048,1024]{1,0:T(8,128)(2,1)}, bf16[2048,1024]{1,0:T(8,128)(2,1)}, bf16[2048,1024]{1,0:T(8,128)(2,1)}, f32[2048,1024]{1,0:T(8,128)}, bf1...) custom-call(s32[1]{0:T(128)} %bitcast.1.at_ref, ...), custom_call_target="tpu_custom_call" | custom-call | tf_op jit(solution)/shard_map/scan_forward/pallas_call | solution.py:334
  121.3 4.5 %fusion.69 = f32[2048,1024]{1,0:T(8,128)S(1)} fusion(bf16[2048,1024]{1,0:T(8,128)(2,1)S(1)} %copy-done.6, bf16[1024,1024]{1,0:T(8,128)(2,1)S(1)} %copy-done), kind=kOutput, calls=%fused_computation.186 | convolution fusion | flops 4294967296 | bytes 14680064 | tf_op jit(solution)/shard_map/dot_general | solution.py:24
  129.0 6.0 %fusion.24 = bf16[1024,1024]{1,0:T(8,128)(2,1)} fusion(bf16[2048,1024]{1,0:T(8,128)(2,1)S(1)} %copy-done.6, bf16[1024,1024]{1,0:T(8,128)(2,1)S(1)} %broadcast_multiply_fusion, bf16[1024,1024]{1,0:T(8,128)(2,1)S(1)} %copy-done.17, f32[2048]{0:T(1024)S(1)} %get-tuple-element.170), kind=kOutput, calls=%fused_computation.50 | convolution fusion | flops 4308598784 | bytes 10493952 | tf_op jit(solution)/shard_map/dot_general | solution.py:43
  135.0 8.4 %multiply_reduce_fusion = (f32[1024]{0:T(1024)S(1)}, f32[2048,1024]{1,0:T(8,128)}) fusion(bf16[2048,1024]{1,0:T(8,128)(2,1)S(1)} %copy-done.6, f32[1024,1024]{1,0:T(8,128)S(1)} %fusion.68, f32[1024,1024]{1,0:T(8,128)S(1)} %copy-done.5, f32[2048]{0:T(1024)S(1)} %get-tuple-element.170, bf16[2048,1024]{1,0:T(8,128)(2,1)} %get-tuple-element.50, ...), kind=kLoop, calls=%fused_computation.5 | loop fusion | flops 25164800 | bytes 25190400 | tf_op jit(solution)/shard_map/reduce_sum | solution.py:567
  143.4 13.3 %multiply_reduce_fusion.2 = (f32[1024]{0:T(1024)S(1)}, bf16[1024,1024]{0,1:T(8,128)(2,1)}) fusion(bf16[1024,1024]{0,1:T(8,128)(2,1)} %copy.84, bf16[2048,1024]{1,0:T(8,128)(2,1)} %get-tuple-element.49, f32[2048]{0:T(1024)S(1)} %get-tuple-element.171, bf16[2048,1024]{1,0:T(8,128)(2,1)} %get-tuple-element.48, f32[2048]{0:T(1024)S(1)} %get-tuple-element.170, ...), kind=kOutput, calls=%fused_computation.41 | convolution fusion | flops 4328520704 | bytes 25190400 | tf_op jit(solution)/shard_map/dot_general | solution.py:43
  156.7 79.8 %scan_backward.1 = (bf16[2048,1408]{1,0:T(8,128)(2,1)}, f32[48,1024]{1,0:T(8,128)}, f32[40,256]{1,0:T(8,128)}, f32[16,128]{1,0:T(8,128)}) custom-call(s32[1]{0:T(128)} %bitcast.1.at_ref, f32[2048,1024]{1,0:T(8,128)} %get-tuple-element.51.dy_ref, f32[2048,1024]{1,0:T(8,128)} %get-tuple-element.52.xc_ref, bf16[2048,1024]{1,0:T(8,128)(2,1)} %get-tuple-element.53.sp_ref, ...), custom_call_target="tpu_custom_call" | custom-call | tf_op jit(solution)/shard_map/scan_backward/pallas_call | solution.py:385
  236.5 9.9 %fusion.22 = f32[1024,1408]{1,0:T(8,128)S(1)} fusion(bf16[2048,1408]{1,0:T(8,128)(2,1)} %get-tuple-element.61, bf16[1024,1024]{1,0:T(8,128)(2,1)} %copy-done.15, bf16[1024,1024]{1,0:T(8,128)(2,1)S(1)} %copy-done.14), kind=kOutput, calls=%fused_computation.45 | convolution fusion | flops 5913968640 | bytes 15728640 | tf_op jit(solution)/shard_map/dot_general | solution.py:43
  250.2 12.0 %fusion.52 = f32[2048,1024]{1,0:T(8,128)} fusion(bf16[1024,1024]{1,0:T(8,128)(2,1)S(1)} %copy-done.12, bf16[2048,1024]{1,0:T(8,128)(2,1)} %get-tuple-element.49, bf16[2048,1024]{1,0:T(8,128)(2,1)} %get-tuple-element.48, f32[1024,1024]{1,0:T(8,128)} %copy-done.7, f32[1024,1024]{1,0:T(8,128)} %fusion.66, f32[2048]{0:T(1024)S(1)} %get-tuple-element.171, ...), kind=kOutput, calls=%fused_computation.174 | convolution fusion | flops 4315938816 | bytes 27283456 | tf_op jit(solution)/shard_map/dot_general | solution.py:28
  272.9 10.0 %convolution_add_fusion = f32[2048,1024]{1,0:T(8,128)S(1)} fusion(f32[2048,1024]{1,0:T(8,128)} %fusion.52, bf16[2048,1408]{1,0:T(8,128)(2,1)} %get-tuple-element.61, bf16[1024,16]{1,0:T(8,128)(2,1)S(1)} %copy.78, bf16[1024,128]{1,0:T(8,128)(2,1)S(1)} %copy-done.23, bf16[1024,128]{1,0:T(8,128)(2,1)S(1)} %copy-done.26, bf16[1024,1024]{1,0:T(8,128)(2,1)S(1)} %copy-done.20), kind=kOutput, calls=%fused_computation.43 | convolution fusion | flops 5922095104 | bytes 25198592 | tf_op jit(solution)/shard_map/dot_general | solution.py:28
  282.9 3.3 copy-done.8
  291.7 43.0 %collective-permute-done.9 = f32[21,128]{1,0:T(8,128)S(1)} collective-permute-done((f32[21,128]{1,0:T(8,128)S(1)}, f32[21,128]{1,0:T(8,128)S(1)}, u32[]{:S(2)}, u32[]{:S(2)}) %collective-permute-start.9) | collective-permute-done | bytes 10784 | tf_op jit(solution)/shard_map/ppermute | solution.py:442
  338.7 3.4 convert_add_fusion.1
  342.1 3.7 collective-permute-done.19
  347.6 4.0 collective-permute-done.20
  353.4 6.6 %collective-permute-done.21 = f32[64,384]{1,0:T(8,128)S(1)} collective-permute-done((f32[64,384]{1,0:T(8,128)S(1)}, f32[64,384]{1,0:T(8,128)S(1)}, u32[]{:S(2)}, u32[]{:S(2)}) %collective-permute-start.21) | collective-permute-done | bytes 98336 | tf_op jit(solution)/shard_map/ppermute | solution.py:442
  364.5 3.7 collective-permute-done.12
  371.7 3.8 collective-permute-done.13
  375.5 3.4 collective-permute-start.14
  379.4 4.4 collective-permute-start.25
  388.5 10.2 %collective-permute-done.15 = bf16[128,1024]{1,0:T(8,128)(2,1)S(1)} collective-permute-done((bf16[128,1024]{1,0:T(8,128)(2,1)S(1)}, bf16[128,1024]{1,0:T(8,128)(2,1)S(1)}, u32[]{:S(2)}, u32[]{:S(2)}) %collective-permute-start.15) | collective-permute-done | bytes 262176 | tf_op jit(solution)/shard_map/ppermute | solution.py:442
  398.9 6.5 %collective-permute-start.16 = (bf16[256,1024]{1,0:T(8,128)(2,1)S(1)}, bf16[256,1024]{1,0:T(8,128)(2,1)S(1)}, u32[]{:S(2)}, u32[]{:S(2)}) collective-permute-start(bf16[256,1024]{1,0:T(8,128)(2,1)S(1)} %pad_maximum_fusion.5), channel_id=1, source_target_pairs={{0,4},{2,6},{4,0},{6,2},{8,12},{10,14},{12,8},{14,10},{16,20},{18,... | collective-permute-start | bytes 1572872 | tf_op jit(solution)/shard_map/ppermute | solution.py:442
  405.4 3.8 fusion.14
  409.2 3.4 collective-permute-done.16
  414.0 6.6 %fusion.13 = (bf16[1024,1024]{1,0:T(8,128)(2,1)}, bf16[1024,1024]{1,0:T(8,128)(2,1)}) fusion(bf16[1024,1024]{1,0:T(8,128)(2,1)S(1)} %copy-done.4, bf16[1024,1024]{1,0:T(8,128)(2,1)} %param.37, bf16[1024,1024]{1,0:T(8,128)(2,1)} %collective-permute-done.4, f32[2048,1024]{1,0:T(8,128)S(1)} %bitcast.77, f32[1024]{0:T(1024)S(1)} %broadcast_multiply_fusion.2, ...), kind=kLoop, calls=%fused_computation.29 | loop fusion | flops 16777216 | bytes 20992000 | tf_op jit(solution)/shard_map/convert_element_type | solution.py:617
  420.6 4.2 convert_element_type.222
  (267 shorter events, 96.6 us)
Async XLA Ops:
  7.2 40.6 %copy-start = (bf16[1024,1024]{1,0:T(8,128)(2,1)S(1)}, bf16[1024,1024]{1,0:T(8,128)(2,1)}, u32[]{:S(2)}) copy-start(bf16[1024,1024]{1,0:T(8,128)(2,1)} %param.36) | copy-start | bytes 6291460
  7.2 413.4 %all-reduce.11.cloned.1.call-start = ((), (), s32[]{:S(2)}) async-start(), calls=%async_computation | async-start | bytes 8388608 | tf_op jit(solution)/shard_map/psum | solution.py:575
  7.3 50.6 %collective-permute-start = (bf16[1024,1024]{1,0:T(8,128)(2,1)}, bf16[1024,1024]{1,0:T(8,128)(2,1)}, u32[]{:S(2)}, u32[]{:S(2)}) collective-permute-start(bf16[1024,1024]{1,0:T(8,128)(2,1)} %param.19), channel_id=1, source_target_pairs={{0,1},{1,0},{2,3},{3,2},{4,5},{5,4},{6,7},{7,6},{8,9},{9,8},{10,11... | collective-permute-start | bytes 6291464 | tf_op jit(solution)/shard_map/ppermute | solution.py:504
  57.9 54.7 %collective-permute-start.1 = (bf16[1024,1024]{1,0:T(8,128)(2,1)}, bf16[1024,1024]{1,0:T(8,128)(2,1)}, u32[]{:S(2)}, u32[]{:S(2)}) collective-permute-start(bf16[1024,1024]{1,0:T(8,128)(2,1)} %param.37), channel_id=1, source_target_pairs={{0,1},{1,0},{2,3},{3,2},{4,5},{5,4},{6,7},{7,6},{8,9},{9,8},{10,11... | collective-permute-start | bytes 6291464 | tf_op jit(solution)/shard_map/ppermute | solution.py:504
  116.8 18.2 %copy-start.7 = (f32[1024,1024]{1,0:T(8,128)}, f32[1024,1024]{1,0:T(8,128)S(1)}, u32[]{:S(2)}) copy-start(f32[1024,1024]{1,0:T(8,128)S(1)} %fusion.68) | copy-start | bytes 12582916
  119.1 8.5 %collective-permute-start.2 = (f32[2,2048]{1,0:T(2,128)S(1)}, f32[2,2048]{1,0:T(2,128)S(1)}, u32[]{:S(2)}, u32[]{:S(2)}) collective-permute-start(f32[2,2048]{1,0:T(2,128)S(1)} %pad_maximum_fusion.11), channel_id=1, source_target_pairs={{0,1},{1,0},{2,3},{3,2},{4,5},{5,4},{6,7},{7,6},{8,9},{9,8},{10,11... | collective-permute-start | bytes 49160 | tf_op jit(solution)/shard_map/ppermute | solution.py:442
  127.6 286.4 %collective-permute-start.3 = (bf16[1024,1024]{1,0:T(8,128)(2,1)}, bf16[1024,1024]{1,0:T(8,128)(2,1)}, u32[]{:S(2)}, u32[]{:S(2)}) collective-permute-start(bf16[1024,1024]{1,0:T(8,128)(2,1)} %slice.379), channel_id=1, source_target_pairs={{0,1},{1,0},{2,3},{3,2},{4,5},{5,4},{6,7},{7,6},{8,9},{9,8},{10,11... | collective-permute-start | bytes 6291464 | tf_op jit(solution)/shard_map/ppermute | solution.py:513
  249.8 12.4 %collective-permute-start.5 = (f32[72,128]{1,0:T(8,128)S(1)}, f32[72,128]{1,0:T(8,128)S(1)}, u32[]{:S(2)}, u32[]{:S(2)}) collective-permute-start(f32[72,128]{1,0:T(8,128)S(1)} %pad_bitcast_fusion), channel_id=1, source_target_pairs={{0,2},{2,0},{4,6},{6,4},{8,10},{10,8},{12,14},{14,12},{16,18},{18,... | collective-permute-start | bytes 110600 | tf_op jit(solution)/shard_map/ppermute | solution.py:442
  262.2 4.0 collective-permute-start.6
  266.3 4.0 collective-permute-start.7
  268.9 65.9 %collective-permute-start.18 = (f32[512,384]{1,0:T(8,128)}, f32[512,384]{1,0:T(8,128)}, u32[]{:S(2)}, u32[]{:S(2)}) collective-permute-start(f32[512,384]{1,0:T(8,128)} %slice_select_fusion), channel_id=1, source_target_pairs={{0,2},{2,0},{4,6},{6,4},{8,10},{10,8},{12,14},{14,12},{16,18},{18,... | collective-permute-start | bytes 2359304 | tf_op jit(solution)/shard_map/ppermute | solution.py:442
  268.9 69.8 %collective-permute-start.10 = (bf16[512,1024]{1,0:T(8,128)(2,1)S(1)}, bf16[512,1024]{1,0:T(8,128)(2,1)}, u32[]{:S(2)}, u32[]{:S(2)}) collective-permute-start(bf16[512,1024]{1,0:T(8,128)(2,1)S(1)} %select_convert_fusion), channel_id=1, source_target_pairs={{0,2},{2,0},{4,6},{6,4},{8,10},{10,8},{12,14},{14,12},{16,18},{18,... | collective-permute-start | bytes 3145736 | tf_op jit(solution)/shard_map/ppermute | solution.py:442
  270.3 18.3 %collective-permute-start.8 = (f32[72,128]{1,0:T(8,128)S(1)}, f32[72,128]{1,0:T(8,128)S(1)}, u32[]{:S(2)}, u32[]{:S(2)}) collective-permute-start(f32[72,128]{1,0:T(8,128)S(1)} %add.153), channel_id=1, source_target_pairs={{0,16},{2,18},{4,20},{6,22},{8,24},{10,26},{12,28},{14,30},{16,0},... | collective-permute-start | bytes 110600 | tf_op jit(solution)/shard_map/ppermute | solution.py:442
  287.8 117.6 %collective-permute-start.4 = (bf16[1024,1024]{1,0:T(8,128)(2,1)}, bf16[1024,1024]{1,0:T(8,128)(2,1)}, u32[]{:S(2)}, u32[]{:S(2)}) collective-permute-start(bf16[1024,1024]{1,0:T(8,128)(2,1)} %slice.378), channel_id=1, source_target_pairs={{0,1},{1,0},{2,3},{3,2},{4,5},{5,4},{6,7},{7,6},{8,9},{9,8},{10,11... | collective-permute-start | bytes 6291464 | tf_op jit(solution)/shard_map/ppermute | solution.py:513
  288.6 46.1 %collective-permute-start.9 = (f32[21,128]{1,0:T(8,128)S(1)}, f32[21,128]{1,0:T(8,128)S(1)}, u32[]{:S(2)}, u32[]{:S(2)}) collective-permute-start(f32[21,128]{1,0:T(8,128)S(1)} %slice.258), channel_id=1, source_target_pairs={{0,1},{1,0},{2,3},{3,2},{4,5},{5,4},{6,7},{7,6},{8,9},{9,8},{10,11... | collective-permute-start | bytes 32264 | tf_op jit(solution)/shard_map/ppermute | solution.py:442
  336.5 9.2 %collective-permute-start.19 = (f32[256,384]{1,0:T(8,128)S(1)}, f32[256,384]{1,0:T(8,128)S(1)}, u32[]{:S(2)}, u32[]{:S(2)}) collective-permute-start(f32[256,384]{1,0:T(8,128)S(1)} %slice_select_fusion.1), channel_id=1, source_target_pairs={{0,4},{2,6},{4,0},{6,2},{8,12},{10,14},{12,8},{14,10},{16,20},{18,... | collective-permute-start | bytes 1179656 | tf_op jit(solution)/shard_map/ppermute | solution.py:442
  345.9 5.8 %collective-permute-start.20 = (f32[128,384]{1,0:T(8,128)S(1)}, f32[128,384]{1,0:T(8,128)S(1)}, u32[]{:S(2)}, u32[]{:S(2)}) collective-permute-start(f32[128,384]{1,0:T(8,128)S(1)} %slice_select_fusion.2), channel_id=1, source_target_pairs={{0,8},{2,10},{4,12},{6,14},{8,0},{10,2},{12,4},{14,6},{16,24},{18,... | collective-permute-start | bytes 589832 | tf_op jit(solution)/shard_map/ppermute | solution.py:442
  346.0 15.0 %collective-permute-start.11 = (bf16[256,1024]{1,0:T(8,128)(2,1)S(1)}, bf16[256,1024]{1,0:T(8,128)(2,1)S(1)}, u32[]{:S(2)}, u32[]{:S(2)}) collective-permute-start(bf16[256,1024]{1,0:T(8,128)(2,1)S(1)} %select_convert_fusion.1), channel_id=1, source_target_pairs={{0,4},{2,6},{4,0},{6,2},{8,12},{10,14},{12,8},{14,10},{16,20},{18,... | collective-permute-start | bytes 1572872 | tf_op jit(solution)/shard_map/ppermute | solution.py:442
  351.7 8.3 %collective-permute-start.21 = (f32[64,384]{1,0:T(8,128)S(1)}, f32[64,384]{1,0:T(8,128)S(1)}, u32[]{:S(2)}, u32[]{:S(2)}) collective-permute-start(f32[64,384]{1,0:T(8,128)S(1)} %slice_select_fusion.3), channel_id=1, source_target_pairs={{0,16},{2,18},{4,20},{6,22},{8,24},{10,26},{12,28},{14,30},{16,0},... | collective-permute-start | bytes 294920 | tf_op jit(solution)/shard_map/ppermute | solution.py:442
  360.1 4.3 collective-permute-start.22
  361.3 6.9 %collective-permute-start.12 = (bf16[128,1024]{1,0:T(8,128)(2,1)S(1)}, bf16[128,1024]{1,0:T(8,128)(2,1)S(1)}, u32[]{:S(2)}, u32[]{:S(2)}) collective-permute-start(bf16[128,1024]{1,0:T(8,128)(2,1)S(1)} %select_convert_fusion.2), channel_id=1, source_target_pairs={{0,8},{2,10},{4,12},{6,14},{8,0},{10,2},{12,4},{14,6},{16,24},{18,... | collective-permute-start | bytes 786440 | tf_op jit(solution)/shard_map/ppermute | solution.py:442
  364.4 41.0 %copy-start.4 = (bf16[1024,1024]{1,0:T(8,128)(2,1)S(1)}, bf16[1024,1024]{1,0:T(8,128)(2,1)}, u32[]{:S(2)}) copy-start(bf16[1024,1024]{1,0:T(8,128)(2,1)} %param.19) | copy-start | bytes 6291460
  364.4 7.1 %collective-permute-start.23 = (bf16[64,384]{1,0:T(8,128)(2,1)S(1)}, bf16[64,384]{1,0:T(8,128)(2,1)S(1)}, u32[]{:S(2)}, u32[]{:S(2)}) collective-permute-start(bf16[64,384]{1,0:T(8,128)(2,1)S(1)} %pad_maximum_fusion.10), channel_id=1, source_target_pairs={{0,16},{2,18},{4,20},{6,22},{8,24},{10,26},{12,28},{14,30},{16,0},... | collective-permute-start | bytes 147464 | tf_op jit(solution)/shard_map/ppermute | solution.py:442
  368.4 7.1 %collective-permute-start.13 = (bf16[64,1024]{1,0:T(8,128)(2,1)S(1)}, bf16[64,1024]{1,0:T(8,128)(2,1)S(1)}, u32[]{:S(2)}, u32[]{:S(2)}) collective-permute-start(bf16[64,1024]{1,0:T(8,128)(2,1)S(1)} %select_convert_fusion.3), channel_id=1, source_target_pairs={{0,16},{2,18},{4,20},{6,22},{8,24},{10,26},{12,28},{14,30},{16,0},... | collective-permute-start | bytes 393224 | tf_op jit(solution)/shard_map/ppermute | solution.py:442
  371.6 7.7 %collective-permute-start.24 = (bf16[128,384]{1,0:T(8,128)(2,1)S(1)}, bf16[128,384]{1,0:T(8,128)(2,1)S(1)}, u32[]{:S(2)}, u32[]{:S(2)}) collective-permute-start(bf16[128,384]{1,0:T(8,128)(2,1)S(1)} %pad_maximum_fusion.9), channel_id=1, source_target_pairs={{0,8},{2,10},{4,12},{6,14},{8,0},{10,2},{12,4},{14,6},{16,24},{18,... | collective-permute-start | bytes 294920 | tf_op jit(solution)/shard_map/ppermute | solution.py:442
  375.5 10.8 %collective-permute-start.14 = (bf16[64,1024]{1,0:T(8,128)(2,1)S(1)}, bf16[64,1024]{1,0:T(8,128)(2,1)S(1)}, u32[]{:S(2)}, u32[]{:S(2)}) collective-permute-start(bf16[64,1024]{1,0:T(8,128)(2,1)S(1)} %add_convert_fusion), channel_id=1, source_target_pairs={{0,16},{2,18},{4,20},{6,22},{8,24},{10,26},{12,28},{14,30},{16,0},... | collective-permute-start | bytes 393224 | tf_op jit(solution)/shard_map/ppermute | solution.py:442
  379.4 8.3 %collective-permute-start.25 = (bf16[256,384]{1,0:T(8,128)(2,1)S(1)}, bf16[256,384]{1,0:T(8,128)(2,1)S(1)}, u32[]{:S(2)}, u32[]{:S(2)}) collective-permute-start(bf16[256,384]{1,0:T(8,128)(2,1)S(1)} %pad_maximum_fusion.8), channel_id=1, source_target_pairs={{0,4},{2,6},{4,0},{6,2},{8,12},{10,14},{12,8},{14,10},{16,20},{18,... | collective-permute-start | bytes 589832 | tf_op jit(solution)/shard_map/ppermute | solution.py:442
  386.4 12.4 %collective-permute-start.15 = (bf16[128,1024]{1,0:T(8,128)(2,1)S(1)}, bf16[128,1024]{1,0:T(8,128)(2,1)S(1)}, u32[]{:S(2)}, u32[]{:S(2)}) collective-permute-start(bf16[128,1024]{1,0:T(8,128)(2,1)S(1)} %pad_maximum_fusion.7), channel_id=1, source_target_pairs={{0,8},{2,10},{4,12},{6,14},{8,0},{10,2},{12,4},{14,6},{16,24},{18,... | collective-permute-start | bytes 786440 | tf_op jit(solution)/shard_map/ppermute | solution.py:442
  387.7 26.2 %slice-start.2 = ((s8[8388608]{0:T(1024)(128)(4,1)}), s8[4194304]{0:T(1024)(128)(4,1)S(1)}, s32[]{:S(2)}) async-start(s8[8388608]{0:T(1024)(128)(4,1)} %bitcast.76), calls=%async_computation.3 | async-start | bytes 8388608
  388.5 39.3 %collective-permute-start.26 = (bf16[512,384]{1,0:T(8,128)(2,1)}, bf16[512,384]{1,0:T(8,128)(2,1)}, u32[]{:S(2)}, u32[]{:S(2)}) collective-permute-start(bf16[512,384]{1,0:T(8,128)(2,1)} %pad_maximum_fusion.6), channel_id=1, source_target_pairs={{0,2},{2,0},{4,6},{6,4},{8,10},{10,8},{12,14},{14,12},{16,18},{18,... | collective-permute-start | bytes 1179656 | tf_op jit(solution)/shard_map/ppermute | solution.py:442
  398.9 13.7 %collective-permute-start.16 = (bf16[256,1024]{1,0:T(8,128)(2,1)S(1)}, bf16[256,1024]{1,0:T(8,128)(2,1)S(1)}, u32[]{:S(2)}, u32[]{:S(2)}) collective-permute-start(bf16[256,1024]{1,0:T(8,128)(2,1)S(1)} %pad_maximum_fusion.5), channel_id=1, source_target_pairs={{0,4},{2,6},{4,0},{6,2},{8,12},{10,14},{12,8},{14,10},{16,20},{18,... | collective-permute-start | bytes 1572872 | tf_op jit(solution)/shard_map/ppermute | solution.py:442
  413.9 17.0 %collective-permute-start.17 = (bf16[512,1024]{1,0:T(8,128)(2,1)}, bf16[512,1024]{1,0:T(8,128)(2,1)}, u32[]{:S(2)}, u32[]{:S(2)}) collective-permute-start(bf16[512,1024]{1,0:T(8,128)(2,1)} %pad_maximum_fusion.4), channel_id=1, source_target_pairs={{0,2},{2,0},{4,6},{6,4},{8,10},{10,8},{12,14},{14,12},{16,18},{18,... | collective-permute-start | bytes 3145736 | tf_op jit(solution)/shard_map/ppermute | solution.py:442
  (38 other events, 240.3 us)
Sparse Core Ops, SparseCore 0:
  288.7 122.4 all-reduce.10

commit v2 on v1

--- a/solution.py
+++ b/solution.py
@@ -454,28 +454,39 @@
     return value
 
 
-def sum_large(values, axis, middle):
+def halves(low, high, axis, bit):
+    upper = (lax.axis_index(axis) & bit) > 0
+    other = swap(jnp.where(upper, low, high).astype(BF16), axis, lax.axis_size(axis), bit)
+    return jnp.where(upper, high, low) + other.astype(F32)
+
+
+def join(value, axis, bit):
+    upper = (lax.axis_index(axis) & bit) > 0
+    other = swap(value, axis, lax.axis_size(axis), bit)
+    return jnp.where(upper, other, value), jnp.where(upper, value, other)
+
+
+def sum_rest(value, axis, held):
     size = lax.axis_size(axis)
-    place = lax.axis_index(axis)
-    kinds = (BF16, F32)
-    for bit in bits(size):
-        upper = (place & bit) > 0
-        halves = []
-        for value, kind in zip(values, kinds):
-            half = value.shape[0] // 2
-            low, high = value[:half], value[half:]
-            other = swap(jnp.where(upper, low, high).astype(kind), axis, size, bit)
-            halves.append(jnp.where(upper, high, low) + other.astype(F32))
-        values = halves
-    values = [value.astype(BF16) for value in middle(values)]
-    for bit in reversed(bits(size)):
-        upper = (place & bit) > 0
-        others = [swap(value, axis, size, bit) for value in values]
-        values = [
-            jnp.concatenate([jnp.where(upper, other, value), jnp.where(upper, value, other)])
-            for value, other in zip(values, others)
-        ]
-    return [value.astype(F32) for value in values]
+    groups = size // 4
+    place = lax.axis_index(axis) // 4
+    half = value.shape[0] // 2
+    value = halves(value[:half], value[half:], axis, 2)
+    rows = half // groups
+
+    def piece(owner):
+        return lax.dynamic_slice_in_dim(value, owner * rows, rows)
+
+    sent = [piece(place ^ offset).astype(BF16) for offset in range(1, groups)]
+    total = piece(place)
+    for offset, member in zip(range(1, groups), sent):
+        total = total + swap(member, axis, size, 4 * offset).astype(F32)
+    total, held = lax.optimization_barrier((total.astype(BF16), held))
+    pieces = [total] + [swap(total, axis, size, 4 * offset) for offset in range(1, groups)]
+    for bit in bits(groups):
+        moved = (place & bit) > 0
+        pieces = [jnp.where(moved, pieces[at ^ bit], pieces[at]) for at in range(groups)]
+    return jnp.concatenate(join(jnp.concatenate(pieces), axis, 2)), held
 
 
 def shards(
@@ -553,7 +564,8 @@
     )
     cot_rest = jnp.concatenate(cot_others) * live_first[rows_own:].astype(BF16)
     cot_all = jnp.concatenate([cot_own, cot_rest])
-    normed_grad = jnp.concatenate([back_own, nt(cot_rest, w_out)])
+    back_rest = nt(cot_rest, w_out)
+    normed_grad = jnp.concatenate([back_own, back_rest])
     gated32 = gated.astype(F32)
     dots = jnp.sum(normed_grad * gated32, axis=1)
     stats = sum_small(jnp.stack([squares[0], reorder(dots)]), ["tensor"])
@@ -561,36 +573,44 @@
     inverse = reorder(lax.rsqrt(stats[0] / inner_width + EPSILON))[:, None]
     lean = inverse**3 * (reorder(stats[1]) / inner_width)[:, None]
 
-    block_out = (tokens.astype(F32) + live_own * inverse[:rows_own] * scatter(branch)).astype(BF16)
+    branch = scatter(branch)
     grad_w_out = tn(gated, (cot_all.astype(F32) * inverse).astype(BF16))
 
-    grad_gate_gain = jnp.sum(normed_grad * gated32 * inverse, axis=0) / gain_gate[0]
     gated_grad = normed_grad * gain_gate * inverse - gated32 * lean / gain_gate
     dy = gated_grad * silu.astype(F32)
     gate_grad = (gated_grad * slope.astype(F32)).astype(BF16)
     normed = jnp.concatenate([normed_own, normed_other])
     grad_w_z = tn(normed, gate_grad)
     early = (grad_w_out.astype(BF16), grad_w_z.astype(BF16))
-    early, dy = lax.optimization_barrier((early, dy))
+    early, dy, gate_grad, back_own, back_rest, gated, inverse = lax.optimization_barrier(
+        (early, dy, gate_grad, back_own, back_rest, gated, inverse)
+    )
+    back = nt(gate_grad, w_z)
+    normed_grad = jnp.concatenate([back_own, back_rest])
+    grad_gate_gain = jnp.sum(normed_grad * gated.astype(F32) * inverse, axis=0) / gain_gate[0]
+    norm_part = jnp.sum(early[1].astype(F32) * w_z.astype(F32), axis=1)
+    dy, back, grad_gate_gain, norm_part = lax.optimization_barrier((dy, back, grad_gate_gain, norm_part))
     early = lax.psum(early, "dp")
 
     cat_grad, gk, gkbc, gh = call_backward(
         at, size, dy, xc, sp, raw, bc, spbc, step, cum, dsig, col, row, states, kx, kbc, hp, expand, fold
     )
-    grad_cat = lax.optimization_barrier(tn(normed, cat_grad))
-
-    def shared_columns(values):
-        part = values[1][:, :double]
-        for bit in bits(size):
-            part = part + swap(part, "tensor", size, bit)
-        return [values[0], jnp.concatenate([part, values[1][:, double:]], axis=1)]
-
-    late, rest = sum_large([grad_cat[:, :width], grad_cat[:, width:]], "dp", shared_columns)
-    back = nt(gate_grad, w_z) + nt(cat_grad, w_cat)
+    early, cat_grad, back, grad_gate_gain, norm_part, branch = lax.optimization_barrier(
+        (early, cat_grad, back, grad_gate_gain, norm_part, branch)
+    )
+    block_out = (tokens.astype(F32) + live_own * inverse[:rows_own] * branch).astype(BF16)
+    grad_cat = tn(normed, cat_grad)
+    half = model_width // 2
+    late = halves(grad_cat[:half], grad_cat[half:], "dp", 1)
+    part = late[:, width : width + double]
+    for bit in bits(size):
+        part = part + swap(part, "tensor", size, bit)
+    late = jnp.concatenate([late[:, :width], part, late[:, width + double :]], axis=1)
+    back = back + nt(cat_grad, w_cat)
+    late, back, grad_cat = lax.optimization_barrier((late, back, grad_cat))
     normed_in_grad = scatter(back)
-
     weighted = grad_cat * w_cat.astype(F32)
-    norm_part = jnp.sum(weighted, axis=1) + jnp.sum(grad_w_z * w_z.astype(F32), axis=1)
+    norm_part = norm_part + jnp.sum(weighted, axis=1)
     gk = gk.reshape(TAPS + 2, 8, width).sum(1)
     gkbc = gkbc.reshape(TAPS + 1, 8, double).sum(1)
     gh = gh.reshape(2, 8, LANES).sum(1)
@@ -600,6 +620,8 @@
     cut = local.shape[0]
     small = jnp.concatenate([local, shared])
     small = jnp.pad(small, (0, -small.shape[0] % 1024)).reshape(-1, LANES)
+    late, (small, normed_in_grad) = sum_rest(late, "dp", (small, normed_in_grad))
+    late = join(late, "dp", 1)
     small = sum_small(small, ["dp"]).reshape(-1)
     local = small[:cut]
     shared = sum_small(small[cut:].reshape(-1, LANES), ["tensor"]).reshape(-1)
@@ -620,10 +642,10 @@
         grad_tokens,
         shared[:model_width],
         early[1].astype(F32),
-        late,
-        rest[:, : double // 2],
-        rest[:, double // 2 : double],
-        rest[:, double : double + heads],
+        jnp.concatenate([member[:, :width] for member in late]).astype(F32),
+        jnp.concatenate([member[:, width : width + double // 2] for member in late]).astype(F32),
+        jnp.concatenate([member[:, width + double // 2 : width + double] for member in late]).astype(F32),
+        jnp.concatenate([member[:, width + double : width + double + heads] for member in late]).astype(F32),
         taps[:TAPS],
         taps[TAPS],
         taps_bc[:TAPS],

time: 452 us -> 456 us (level)
  other arithmetic: 66.4 us -> 94.3 us
  starting transfers between devices: 38.3 us -> 22.1 us
  matrix products: 85.3 us -> 76.1 us
    ppermute x23 -> x17, waiting for transfers between devices: 86.8 us -> 54.4 us  [swap(): lax.ppermute(value, axis, [(place, place ^ bit) for place in range(size)])]
    ppermute x2, waiting for transfers between devices: 0.01 us -> 30.3 us  [scatter(): total = total + lax.ppermute(part, 'tensor', pairs).astype(F32)]
    ppermute x23 -> x17, starting transfers between devices: 34.4 us -> 15.2 us  [swap(): lax.ppermute(value, axis, [(place, place ^ bit) for place in range(size)])]
    add x7 -> x6, other arithmetic: 5.54 us -> 24.1 us  [the longest x1 12.1 us: shards(): back = back + nt(cat_grad, w_cat)]
    mul x1 -> x3, other arithmetic: 0.01 us -> 11.7 us  [the longest x1 11.7 us: shards(): dy = gated_grad * silu.astype(F32)]
    convert_element_type x8, other arithmetic: 3.54 us -> 10.1 us  [the longest x1 3.73 us: shards(): jnp.concatenate([member[:, :width] for member in late]).astype(F32)]
    dot_general x3, matrix products: 29.1 us -> 24.1 us  [tn(): lax.dot_general(left, right, (((0,), (0,)), ((), ())), preferred_element_...]
    unnamed x93 -> x129, local copies, waits for them, and re-layouts: 17.1 us -> 14.6 us
  transfers between devices with their start and end apart: 28 -> 22, of which waited for: 15 -> 13; matrix products, arithmetic and copies ran while one was open for 38% -> 35% of each run, Pallas kernels for 27% -> 26%
where the time goes in v2:
time: 456 us; the launch traced here: 447 us
  Pallas kernels  118 us (26%)
  other arithmetic  94.3 us (21%)
  waiting for transfers between devices  89.7 us (20%)
  matrix products  76.1 us (17%)
  local copies, waits for them, and re-layouts  31.2 us (7%)
  starting transfers between devices  22.1 us (5%)
  between operations  15.4 us (3%)
    pallas_call x1, Pallas kernels, call_backward(): pl.pallas_call(backward_kernel, grid_spec=pltpu.PrefetchScalarGridSpec(nu...  79.8 us
    ppermute x17, waiting for transfers between devices, swap(): lax.ppermute(value, axis, [(place, place ^ bit) for place in range(size)])  54.4 us
    pallas_call x1, Pallas kernels, call_forward(): pl.pallas_call(functools.partial(forward_kernel, per_block), grid_spec=pl...  38.2 us
    ppermute x2, waiting for transfers between devices, scatter(): total = total + lax.ppermute(part, 'tensor', pairs).astype(F32)  30.3 us
    dot_general x5, matrix products, nn(): return jnp.dot(left, right, preferred_element_type=F32)  27.3 us
    dot_general x4, matrix products, nt(): lax.dot_general(left, right, (((1,), (1,)), ((), ())), preferred_element_...  24.7 us
    dot_general x3, matrix products, tn(): lax.dot_general(left, right, (((0,), (0,)), ((), ())), preferred_element_...  24.1 us
    ppermute x17, starting transfers between devices, swap(): lax.ppermute(value, axis, [(place, place ^ bit) for place in range(size)])  15.2 us
  transfers between devices with their start and end apart: 22, of which 13 were waited for; matrix products, arithmetic and copies ran while one was open for 35% of the time, Pallas kernels for 26%

profile of v2, /device:TPU:0, one launch (start us, length us, event | category | flops | bytes accessed | tf_op | source)
XLA Modules:
  0.0 446.8 jit_solution(12596323884810171709)
XLA Ops:
  28.8 3.5 fusion.11
  32.3 3.1 broadcast_multiply_fusion.1
  37.3 6.7 %fusion.65.zmine_ref = f32[1024,1024]{1,0:T(8,128)} fusion(bf16[1024,1024]{1,0:T(8,128)(2,1)} %fusion.11, bf16[1024,1024]{1,0:T(8,128)(2,1)} %param.23), kind=kOutput, calls=%fused_computation.171 | convolution fusion | flops 2147483648 | bytes 8388608 | tf_op jit(solution)/shard_map/dot_general | solution.py:24
  44.1 4.5 %fusion.66 = f32[1024,1024]{1,0:T(8,128)} fusion(bf16[1024,1024]{1,0:T(8,128)(2,1)S(1)} %copy-done.22, bf16[1024,1024]{1,0:T(8,128)(2,1)S(1)} %copy-done), kind=kOutput, calls=%fused_computation.172 | convolution fusion | flops 2147483648 | bytes 8388608 | tf_op jit(solution)/shard_map/dot_general | solution.py:28
  48.6 5.7 %fusion.57.mine_ref = f32[1024,1408]{1,0:T(8,128)} fusion(bf16[1024,1024]{1,0:T(8,128)(2,1)S(1)} %copy-done.19, bf16[1024,16]{1,0:T(8,128)(2,1)S(1)} %copy.84, bf16[1024,128]{1,0:T(8,128)(2,1)S(1)} %copy-done.34, bf16[1024,128]{1,0:T(8,128)(2,1)S(1)} %copy-done.37, bf16[1024,1024]{1,0:T(8,128)(2,1)S(1)} %copy-done.26), kind=kOutput, calls=%fused_computation.164 | convolution fusion | flops 2967207936 | bytes 10518528 | tf_op jit(solution)/shard_map/dot_general | solution.py:24
  62.2 4.4 fusion.67.zother_ref
  66.5 5.9 %fusion.55.other_ref = f32[1024,1408]{1,0:T(8,128)} fusion(bf16[1024,1024]{1,0:T(8,128)(2,1)S(1)} %fusion.8, bf16[1024,16]{1,0:T(8,128)(2,1)S(1)} %copy.84, bf16[1024,128]{1,0:T(8,128)(2,1)S(1)} %copy-done.34, bf16[1024,128]{1,0:T(8,128)(2,1)S(1)} %copy-done.37, bf16[1024,1024]{1,0:T(8,128)(2,1)S(1)} %copy-done.26), kind=kOutput, calls=%fused_computation.163 | convolution fusion | flops 2967207936 | bytes 10518528 | tf_op jit(solution)/shard_map/dot_general | solution.py:24
  73.1 38.2 %scan_forward.1 = (bf16[2048,1024]{1,0:T(8,128)(2,1)}, bf16[2048,1024]{1,0:T(8,128)(2,1)}, bf16[2048,1024]{1,0:T(8,128)(2,1)}, f32[2048,1024]{1,0:T(8,128)}, bf1...) custom-call(s32[1]{0:T(128)} %bitcast.1.at_ref, ...), custom_call_target="tpu_custom_call" | custom-call | tf_op jit(solution)/shard_map/scan_forward/pallas_call | solution.py:334
  121.5 4.6 %fusion.70 = f32[2048,1024]{1,0:T(8,128)S(1)} fusion(bf16[2048,1024]{1,0:T(8,128)(2,1)S(1)} %copy-done.5, bf16[1024,1024]{1,0:T(8,128)(2,1)S(1)} %copy-done), kind=kOutput, calls=%fused_computation.176 | convolution fusion | flops 4294967296 | bytes 14680064 | tf_op jit(solution)/shard_map/dot_general | solution.py:24
  126.1 3.2 copy-done.13
  132.5 11.7 %convert_multiply_fusion.2 = (f32[2048,1024]{1,0:T(8,128)}, bf16[2048,1024]{1,0:T(8,128)(2,1)}) fusion(bf16[2048,1024]{1,0:T(8,128)(2,1)} %get-tuple-element.72, f32[2048]{0:T(1024)S(1)} %get-tuple-element.194, bf16[2048,1024]{1,0:T(8,128)(2,1)S(1)} %copy-done.5, f32[2048]{0:T(1024)S(1)} %get-tuple-element.195, f32[1024]{0:T(1024)S(1)} %convert_element_type.209, ...), kind=kLoop, calls=%fused_computation.9 | loop fusion | flops 25165824 | bytes 33574912 | tf_op jit(solution)/shard_map/mul | solution.py:580
  144.3 8.2 %fusion.26 = bf16[1024,1024]{1,0:T(8,128)(2,1)S(1)} fusion(bf16[2048,1024]{1,0:T(8,128)(2,1)} %get-tuple-element.77, bf16[1024,1024]{1,0:T(8,128)(2,1)} %copy-done.21, bf16[1024,1024]{1,0:T(8,128)(2,1)} %fusion.11), kind=kOutput, calls=%fused_computation.52 | convolution fusion | flops 4304404480 | bytes 10485760 | tf_op jit(solution)/shard_map/dot_general | solution.py:43
  152.5 6.0 %fusion.25 = bf16[1024,1024]{1,0:T(8,128)(2,1)} fusion(bf16[2048,1024]{1,0:T(8,128)(2,1)S(1)} %copy-done.5, bf16[1024,1024]{1,0:T(8,128)(2,1)S(1)} %copy-done.25, bf16[1024,1024]{1,0:T(8,128)(2,1)S(1)} %copy-done.23, f32[2048]{0:T(1024)S(1)} %get-tuple-element.195), kind=kOutput, calls=%fused_computation.51 | convolution fusion | flops 4308598784 | bytes 10493952 | tf_op jit(solution)/shard_map/dot_general | solution.py:43
  161.4 16.2 %collective-permute-done.3 = bf16[1024,1024]{1,0:T(8,128)(2,1)} collective-permute-done((bf16[1024,1024]{1,0:T(8,128)(2,1)}, bf16[1024,1024]{1,0:T(8,128)(2,1)}, u32[]{:S(2)}, u32[]{:S(2)}) %collective-permute-start.3) | collective-permute-done | bytes 2097184 | tf_op jit(solution)/shard_map/ppermute | solution.py:524
  177.6 6.0 %slice_add_fusion = f32[1024,1024]{1,0:T(8,128)} fusion(f32[2048,1024]{1,0:T(8,128)} %copy-done.13, bf16[1024,1024]{1,0:T(8,128)(2,1)} %collective-permute-done.3), kind=kLoop, calls=%fused_computation.36 | loop fusion | flops 2097152 | bytes 10485760 | tf_op jit(solution)/shard_map/add | solution.py:524
  183.6 3.7 fusion.4
  188.0 7.1 %fusion.69 = f32[2048,1024]{1,0:T(8,128)} fusion(bf16[2048,1024]{1,0:T(8,128)(2,1)S(1)} %copy-done.14, bf16[1024,1024]{1,0:T(8,128)(2,1)S(1)} %copy-done.18), kind=kOutput, calls=%fused_computation.175 | convolution fusion | flops 4294967296 | bytes 14680064 | tf_op jit(solution)/shard_map/dot_general | solution.py:28
  195.0 79.8 %scan_backward.1 = (bf16[2048,1408]{1,0:T(8,128)(2,1)}, f32[48,1024]{1,0:T(8,128)}, f32[40,256]{1,0:T(8,128)}, f32[16,128]{1,0:T(8,128)}) custom-call(s32[1]{0:T(128)} %bitcast.1.at_ref, f32[2048,1024]{1,0:T(8,128)} %get-tuple-element.81.dy_ref, f32[2048,1024]{1,0:T(8,128)} %get-tuple-element.82.xc_ref, bf16[2048,1024]{1,0:T(8,128)(2,1)} %get-tuple-element.83.sp_ref, ...), custom_call_target="tpu_custom_call" | custom-call | tf_op jit(solution)/shard_map/scan_backward/pallas_call | solution.py:385
  277.3 9.9 %fusion.23 = f32[1024,1408]{1,0:T(8,128)S(1)} fusion(bf16[2048,1408]{1,0:T(8,128)(2,1)} %get-tuple-element.96, bf16[1024,1024]{1,0:T(8,128)(2,1)} %copy-done.21, bf16[1024,1024]{1,0:T(8,128)(2,1)S(1)} %copy-done.20), kind=kOutput, calls=%fused_computation.48 | convolution fusion | flops 5913968640 | bytes 15728640 | tf_op jit(solution)/shard_map/dot_general | solution.py:43
  294.6 3.1 convert_add_fusion.2
  299.2 10.7 %fusion.53 = f32[2048,1024]{1,0:T(8,128)} fusion(bf16[2048,1408]{1,0:T(8,128)(2,1)} %get-tuple-element.96, bf16[1024,16]{1,0:T(8,128)(2,1)S(1)} %copy-done.30, bf16[1024,128]{1,0:T(8,128)(2,1)S(1)} %copy-done.35, bf16[1024,128]{1,0:T(8,128)(2,1)S(1)} %copy-done.38, bf16[1024,1024]{1,0:T(8,128)(2,1)S(1)} %copy-done.27), kind=kOutput, calls=%fused_computation.162 | convolution fusion | flops 5919997952 | bytes 16809984 | tf_op jit(solution)/shard_map/dot_general | solution.py:28
  310.0 12.1 %add.153 = f32[2048,1024]{1,0:T(8,128)} add(f32[2048,1024]{1,0:T(8,128)} %fusion.69, f32[2048,1024]{1,0:T(8,128)} %fusion.53) | non-fusion elementwise | flops 2097152 | bytes 25165824 | tf_op jit(solution)/shard_map/add | solution.py:609
  328.8 12.3 %collective-permute-done.6 = bf16[256,1408]{1,0:T(8,128)(2,1)S(1)} collective-permute-done((bf16[256,1408]{1,0:T(8,128)(2,1)S(1)}, bf16[256,1408]{1,0:T(8,128)(2,1)S(1)}, u32[]{:S(2)}, u32[]{:S(2)}) %collective-permute-start.6) | collective-permute-done | bytes 720928 | tf_op jit(solution)/shard_map/ppermute | solution.py:442
  345.8 4.9 %collective-permute-done.9 = bf16[64,1408]{1,0:T(8,128)(2,1)S(1)} collective-permute-done((bf16[64,1408]{1,0:T(8,128)(2,1)S(1)}, bf16[64,1408]{1,0:T(8,128)(2,1)S(1)}, u32[]{:S(2)}, u32[]{:S(2)}) %collective-permute-start.9) | collective-permute-done | bytes 180256 | tf_op jit(solution)/shard_map/ppermute | solution.py:442
  350.7 8.5 %collective-permute-done.8 = bf16[64,1408]{1,0:T(8,128)(2,1)S(1)} collective-permute-done((bf16[64,1408]{1,0:T(8,128)(2,1)S(1)}, bf16[64,1408]{1,0:T(8,128)(2,1)S(1)}, u32[]{:S(2)}, u32[]{:S(2)}) %collective-permute-start.8) | collective-permute-done | bytes 180256 | tf_op jit(solution)/shard_map/ppermute | solution.py:442
  359.4 14.1 %collective-permute-done.10 = bf16[1024,1024]{1,0:T(8,128)(2,1)S(1)} collective-permute-done((bf16[1024,1024]{1,0:T(8,128)(2,1)S(1)}, bf16[1024,1024]{1,0:T(8,128)(2,1)S(1)}, u32[]{:S(2)}, u32[]{:S(2)}) %collective-permute-start.10) | collective-permute-done | bytes 2097184 | tf_op jit(solution)/shard_map/ppermute | solution.py:524
  380.6 4.9 %collective-permute-done.16 = bf16[64,1408]{1,0:T(8,128)(2,1)S(1)} collective-permute-done((bf16[64,1408]{1,0:T(8,128)(2,1)S(1)}, bf16[64,1408]{1,0:T(8,128)(2,1)S(1)}, u32[]{:S(2)}, u32[]{:S(2)}) %collective-permute-start.16) | collective-permute-done | bytes 180256 | tf_op jit(solution)/shard_map/ppermute | solution.py:442
  385.5 8.5 %collective-permute-done.17 = bf16[64,1408]{1,0:T(8,128)(2,1)S(1)} collective-permute-done((bf16[64,1408]{1,0:T(8,128)(2,1)S(1)}, bf16[64,1408]{1,0:T(8,128)(2,1)S(1)}, u32[]{:S(2)}, u32[]{:S(2)}) %collective-permute-start.17) | collective-permute-done | bytes 180256 | tf_op jit(solution)/shard_map/ppermute | solution.py:442
  402.9 9.1 %collective-permute-done.12 = f32[72,128]{1,0:T(8,128)S(1)} collective-permute-done((f32[72,128]{1,0:T(8,128)S(1)}, f32[72,128]{1,0:T(8,128)S(1)}, u32[]{:S(2)}, u32[]{:S(2)}) %collective-permute-start.12) | collective-permute-done | bytes 36896 | tf_op jit(solution)/shard_map/ppermute | solution.py:442
  412.0 3.9 collective-permute-done.13
  417.8 4.7 %fusion.15 = (bf16[1024,1024]{1,0:T(8,128)(2,1)}, bf16[1024,1024]{1,0:T(8,128)(2,1)}) fusion(bf16[1024,1024]{1,0:T(8,128)(2,1)S(1)} %copy-done.9, f32[1024,1024]{1,0:T(8,128)S(1)} %copy-done.2, bf16[1024,1024]{1,0:T(8,128)(2,1)} %param.37, f32[1024]{0:T(1024)S(1)} %broadcast_multiply_fusion.2, f32[1024]{0:T(1024)S(1)} %copy-done.52, ...), kind=kLoop, calls=%fused_computation.31 | loop fusion | flops 12582912 | bytes 16797696 | tf_op jit(solution)/shard_map/convert_element_type | solution.py:639
  433.5 3.7 maximum_convert_fusion
  (284 shorter events, 102.5 us)
Async XLA Ops:
  7.2 36.8 %copy-start = (bf16[1024,1024]{1,0:T(8,128)(2,1)S(1)}, bf16[1024,1024]{1,0:T(8,128)(2,1)}, u32[]{:S(2)}) copy-start(bf16[1024,1024]{1,0:T(8,128)(2,1)} %param.36) | copy-start | bytes 6291460
  7.2 49.0 %collective-permute-start = (bf16[1024,1024]{1,0:T(8,128)(2,1)}, bf16[1024,1024]{1,0:T(8,128)(2,1)}, u32[]{:S(2)}, u32[]{:S(2)}) collective-permute-start(bf16[1024,1024]{1,0:T(8,128)(2,1)} %param.19), channel_id=1, source_target_pairs={{0,1},{1,0},{2,3},{3,2},{4,5},{5,4},{6,7},{7,6},{8,9},{9,8},{10,11... | collective-permute-start | bytes 6291464 | tf_op jit(solution)/shard_map/ppermute | solution.py:515
  18.2 17.2 %copy-start.48 = (f32[1024]{0:T(1024)}, f32[1024]{0:T(1024)S(1)}, u32[]{:S(2)}) copy-start(f32[1024]{0:T(1024)S(1)} %get-tuple-element.211) | copy-start | bytes 12292
  19.1 47.4 %copy-start.29 = (bf16[1024,16]{1,0:T(8,128)(2,1)}, bf16[1024,16]{1,0:T(8,128)(2,1)S(1)}, u32[]{:S(2)}) copy-start(bf16[1024,16]{1,0:T(8,128)(2,1)S(1)} %copy.84) | copy-start | bytes 98308
  56.2 55.9 %collective-permute-start.1 = (bf16[1024,1024]{1,0:T(8,128)(2,1)}, bf16[1024,1024]{1,0:T(8,128)(2,1)}, u32[]{:S(2)}, u32[]{:S(2)}) collective-permute-start(bf16[1024,1024]{1,0:T(8,128)(2,1)} %param.37), channel_id=1, source_target_pairs={{0,1},{1,0},{2,3},{3,2},{4,5},{5,4},{6,7},{7,6},{8,9},{9,8},{10,11... | collective-permute-start | bytes 6291464 | tf_op jit(solution)/shard_map/ppermute | solution.py:515
  116.4 16.1 %copy-start.7 = (f32[1024,1024]{1,0:T(8,128)}, f32[1024,1024]{1,0:T(8,128)S(1)}, u32[]{:S(2)}) copy-start(f32[1024,1024]{1,0:T(8,128)S(1)} %fusion.68) | copy-start | bytes 12582916
  120.8 11.7 %collective-permute-start.2 = (f32[2,2048]{1,0:T(2,128)S(1)}, f32[2,2048]{1,0:T(2,128)S(1)}, u32[]{:S(2)}, u32[]{:S(2)}) collective-permute-start(f32[2,2048]{1,0:T(2,128)S(1)} %pad_maximum_fusion.9), channel_id=1, source_target_pairs={{0,1},{1,0},{2,3},{3,2},{4,5},{5,4},{6,7},{7,6},{8,9},{9,8},{10,11... | collective-permute-start | bytes 49160 | tf_op jit(solution)/shard_map/ppermute | solution.py:442
  131.0 46.6 %collective-permute-start.3 = (bf16[1024,1024]{1,0:T(8,128)(2,1)}, bf16[1024,1024]{1,0:T(8,128)(2,1)}, u32[]{:S(2)}, u32[]{:S(2)}) collective-permute-start(bf16[1024,1024]{1,0:T(8,128)(2,1)} %slice.312), channel_id=1, source_target_pairs={{0,1},{1,0},{2,3},{3,2},{4,5},{5,4},{6,7},{7,6},{8,9},{9,8},{10,11... | collective-permute-start | bytes 6291464 | tf_op jit(solution)/shard_map/ppermute | solution.py:524
  160.7 116.6 %all-reduce.11.cloned.1.call-start = ((), (), s32[]{:S(2)}) async-start(), calls=%async_computation | async-start | bytes 8388608 | tf_op jit(solution)/shard_map/psum | solution.py:593
  161.4 22.2 %copy-start.4 = (f32[1024,1024]{1,0:T(8,128)S(1)}, f32[1024,1024]{1,0:T(8,128)}, u32[]{:S(2)}) copy-start(f32[1024,1024]{1,0:T(8,128)} %fusion.66) | copy-start | bytes 12582916
  161.4 22.1 %copy-start.6 = (bf16[2048,1024]{1,0:T(8,128)(2,1)S(1)}, bf16[2048,1024]{1,0:T(8,128)(2,1)}, u32[]{:S(2)}) copy-start(bf16[2048,1024]{1,0:T(8,128)(2,1)} %get-tuple-element.80) | copy-start | bytes 12582916
  195.0 82.3 %copy-start.20 = (bf16[1024,1024]{1,0:T(8,128)(2,1)S(1)}, bf16[1024,1024]{1,0:T(8,128)(2,1)}, u32[]{:S(2)}) copy-start(bf16[1024,1024]{1,0:T(8,128)(2,1)} %fusion.11) | copy-start | bytes 6291460
  291.1 3.4 collective-permute-start.4
  297.7 24.7 %collective-permute-start.5 = (f32[512,256]{1,0:T(8,128)S(1)}, f32[512,256]{1,0:T(8,128)S(1)}, u32[]{:S(2)}, u32[]{:S(2)}) collective-permute-start(f32[512,256]{1,0:T(8,128)S(1)} %slice.231), channel_id=1, source_target_pairs={{0,1},{1,0},{2,3},{3,2},{4,5},{5,4},{6,7},{7,6},{8,9},{9,8},{10,11... | collective-permute-start | bytes 1572872 | tf_op jit(solution)/shard_map/ppermute | solution.py:442
  322.9 18.1 %collective-permute-start.6 = (bf16[256,1408]{1,0:T(8,128)(2,1)S(1)}, bf16[256,1408]{1,0:T(8,128)(2,1)S(1)}, u32[]{:S(2)}, u32[]{:S(2)}) collective-permute-start(bf16[256,1408]{1,0:T(8,128)(2,1)S(1)} %select_convert_fusion.1), channel_id=1, source_target_pairs={{0,4},{2,6},{4,0},{6,2},{8,12},{10,14},{12,8},{14,10},{16,20},{18,... | collective-permute-start | bytes 2162696 | tf_op jit(solution)/shard_map/ppermute | solution.py:442
  325.8 47.6 %collective-permute-start.10 = (bf16[1024,1024]{1,0:T(8,128)(2,1)S(1)}, bf16[1024,1024]{1,0:T(8,128)(2,1)S(1)}, u32[]{:S(2)}, u32[]{:S(2)}) collective-permute-start(bf16[1024,1024]{1,0:T(8,128)(2,1)S(1)} %slice.311), channel_id=1, source_target_pairs={{0,1},{1,0},{2,3},{3,2},{4,5},{5,4},{6,7},{7,6},{8,9},{9,8},{10,11... | collective-permute-start | bytes 6291464 | tf_op jit(solution)/shard_map/ppermute | solution.py:524
  328.7 17.0 %copy-start.50 = (f32[1280]{0:T(1024)S(1)}, f32[1280]{0:T(1024)}, u32[]{:S(2)}) copy-start(f32[1280]{0:T(1024)} %reshape.190) | copy-start | bytes 15364
  341.3 9.4 %collective-permute-start.9 = (bf16[64,1408]{1,0:T(8,128)(2,1)S(1)}, bf16[64,1408]{1,0:T(8,128)(2,1)S(1)}, u32[]{:S(2)}, u32[]{:S(2)}) collective-permute-start(bf16[64,1408]{1,0:T(8,128)(2,1)S(1)} %get-tuple-element.179), channel_id=1, source_target_pairs={{0,24},{2,26},{4,28},{6,30},{8,16},{10,18},{12,20},{14,22},{16,8},... | collective-permute-start | bytes 540680 | tf_op jit(solution)/shard_map/ppermute | solution.py:442
  343.0 16.3 %collective-permute-start.8 = (bf16[64,1408]{1,0:T(8,128)(2,1)S(1)}, bf16[64,1408]{1,0:T(8,128)(2,1)S(1)}, u32[]{:S(2)}, u32[]{:S(2)}) collective-permute-start(bf16[64,1408]{1,0:T(8,128)(2,1)S(1)} %get-tuple-element.180), channel_id=1, source_target_pairs={{0,16},{2,18},{4,20},{6,22},{8,24},{10,26},{12,28},{14,30},{16,0},... | collective-permute-start | bytes 540680 | tf_op jit(solution)/shard_map/ppermute | solution.py:442
  344.1 15.2 %collective-permute-start.7 = (bf16[64,1408]{1,0:T(8,128)(2,1)S(1)}, bf16[64,1408]{1,0:T(8,128)(2,1)S(1)}, u32[]{:S(2)}, u32[]{:S(2)}) collective-permute-start(bf16[64,1408]{1,0:T(8,128)(2,1)S(1)} %get-tuple-element.178), channel_id=1, source_target_pairs={{0,8},{2,10},{4,12},{6,14},{8,0},{10,2},{12,4},{14,6},{16,24},{18,... | collective-permute-start | bytes 540680 | tf_op jit(solution)/shard_map/ppermute | solution.py:442
  359.4 35.9 %copy-start.42 = (f32[1,2048]{1,0:T(1,128)S(1)}, f32[1,2048]{1,0:T(1,128)}, u32[]{:S(2)}) copy-start(f32[1,2048]{1,0:T(1,128)} %copy-done.41) | copy-start | bytes 24580
  359.4 35.9 %copy-start.16 = (bf16[1024,1024]{1,0:T(8,128)(2,1)S(1)}, bf16[1024,1024]{1,0:T(8,128)(2,1)}, u32[]{:S(2)}) copy-start(bf16[1024,1024]{1,0:T(8,128)(2,1)} %get-tuple-element.108) | copy-start | bytes 6291460
  376.2 9.3 %collective-permute-start.16 = (bf16[64,1408]{1,0:T(8,128)(2,1)S(1)}, bf16[64,1408]{1,0:T(8,128)(2,1)S(1)}, u32[]{:S(2)}, u32[]{:S(2)}) collective-permute-start(bf16[64,1408]{1,0:T(8,128)(2,1)S(1)} %add_convert_fusion), channel_id=1, source_target_pairs={{0,24},{2,26},{4,28},{6,30},{8,16},{10,18},{12,20},{14,22},{16,8},... | collective-permute-start | bytes 540680 | tf_op jit(solution)/shard_map/ppermute | solution.py:442
  377.8 16.3 %collective-permute-start.17 = (bf16[64,1408]{1,0:T(8,128)(2,1)S(1)}, bf16[64,1408]{1,0:T(8,128)(2,1)S(1)}, u32[]{:S(2)}, u32[]{:S(2)}) collective-permute-start(bf16[64,1408]{1,0:T(8,128)(2,1)S(1)} %add_convert_fusion), channel_id=1, source_target_pairs={{0,16},{2,18},{4,20},{6,22},{8,24},{10,26},{12,28},{14,30},{16,0},... | collective-permute-start | bytes 540680 | tf_op jit(solution)/shard_map/ppermute | solution.py:442
  378.9 15.2 %collective-permute-start.18 = (bf16[64,1408]{1,0:T(8,128)(2,1)S(1)}, bf16[64,1408]{1,0:T(8,128)(2,1)S(1)}, u32[]{:S(2)}, u32[]{:S(2)}) collective-permute-start(bf16[64,1408]{1,0:T(8,128)(2,1)S(1)} %add_convert_fusion), channel_id=1, source_target_pairs={{0,8},{2,10},{4,12},{6,14},{8,0},{10,2},{12,4},{14,6},{16,24},{18,... | collective-permute-start | bytes 540680 | tf_op jit(solution)/shard_map/ppermute | solution.py:442
  380.6 19.8 %collective-permute-start.11 = (f32[72,128]{1,0:T(8,128)S(1)}, f32[72,128]{1,0:T(8,128)S(1)}, u32[]{:S(2)}, u32[]{:S(2)}) collective-permute-start(f32[72,128]{1,0:T(8,128)S(1)} %pad_bitcast_fusion), channel_id=1, source_target_pairs={{0,2},{2,0},{4,6},{6,4},{8,10},{10,8},{12,14},{14,12},{16,18},{18,... | collective-permute-start | bytes 110600 | tf_op jit(solution)/shard_map/ppermute | solution.py:442
  394.2 22.1 %collective-permute-start.19 = (bf16[256,1408]{1,0:T(8,128)(2,1)S(1)}, bf16[256,1408]{1,0:T(8,128)(2,1)S(1)}, u32[]{:S(2)}, u32[]{:S(2)}) collective-permute-start(bf16[256,1408]{1,0:T(8,128)(2,1)S(1)} %pad_maximum_fusion.8), channel_id=1, source_target_pairs={{0,4},{2,6},{4,0},{6,2},{8,12},{10,14},{12,8},{14,10},{16,20},{18,... | collective-permute-start | bytes 2162696 | tf_op jit(solution)/shard_map/ppermute | solution.py:442
  400.4 11.6 %collective-permute-start.12 = (f32[72,128]{1,0:T(8,128)S(1)}, f32[72,128]{1,0:T(8,128)S(1)}, u32[]{:S(2)}, u32[]{:S(2)}) collective-permute-start(f32[72,128]{1,0:T(8,128)S(1)} %add.165), channel_id=1, source_target_pairs={{0,4},{2,6},{4,0},{6,2},{8,12},{10,14},{12,8},{14,10},{16,20},{18,... | collective-permute-start | bytes 110600 | tf_op jit(solution)/shard_map/ppermute | solution.py:442
  412.0 4.0 collective-permute-start.13
  416.0 6.5 %collective-permute-start.14 = (f32[72,128]{1,0:T(8,128)S(1)}, f32[72,128]{1,0:T(8,128)S(1)}, u32[]{:S(2)}, u32[]{:S(2)}) collective-permute-start(f32[72,128]{1,0:T(8,128)S(1)} %add.167), channel_id=1, source_target_pairs={{0,16},{2,18},{4,20},{6,22},{8,24},{10,26},{12,28},{14,30},{16,0},... | collective-permute-start | bytes 110600 | tf_op jit(solution)/shard_map/ppermute | solution.py:442
  417.8 10.3 %collective-permute-start.20 = (bf16[512,1408]{1,0:T(8,128)(2,1)}, bf16[512,1408]{1,0:T(8,128)(2,1)}, u32[]{:S(2)}, u32[]{:S(2)}) collective-permute-start(bf16[512,1408]{1,0:T(8,128)(2,1)} %pad_maximum_fusion.7), channel_id=1, source_target_pairs={{0,2},{2,0},{4,6},{6,4},{8,10},{10,8},{12,14},{14,12},{16,18},{18,... | collective-permute-start | bytes 4325384 | tf_op jit(solution)/shard_map/ppermute | solution.py:442
  422.5 3.8 collective-permute-start.15
  (51 other events, 315.6 us)
Sparse Core Ops, SparseCore 0:
  165.2 112.0 all-reduce.10
